TPU v7x, 1024 devices: a whole 4x4x32 slice. The times are simulated.
1024 devices in a mesh: dp: 8 (over z_lo), section: 32 (over y, x, core), tensor: 4 (over z_hi).
Axes of the slice: x: 4, y: 4, z: 32 (z_hi: 4, z_lo: 8; z = z_hi * 8 + z_lo), core: 2. Of those that a mesh axis runs over, the one named last changes fastest.
Arguments:
- section_output: bfloat16 [32, 1024, 16384], P('section', 'dp', 'tensor')
- sketch_matrix: bfloat16 [32, 16384, 32], P('section', 'tensor'), may hold values from -0.046875 to 0.046875
- boundary_gain: bfloat16 [32, 16384], P('section', 'tensor'), may hold values from 0.099609375 to 1.8984375
- grad_gained: bfloat16 [32, 1024, 16384], P('section', 'dp', 'tensor')
Outputs:
- grad_output: bfloat16 [32, 1024, 16384], P('section', 'dp', 'tensor')
- gain_grad: float32 [32, 16384], P('section', 'tensor')
All inputs are finite; a program needn't handle non-finite values.
Results may differ from a plain program's by a relative error of at most 0.0074.
Values may be sent and summed in bfloat16 or wider, within the bound.
No kernel may reach another device: no remote copies, remote signals or barrier semaphores. Data moves between devices by JAX's collectives and lax.ppermute only.
A program may use at most 32 MiB of HBM per device.

v0:
```python
import jax
import jax.numpy as jnp
from jax import lax
from jax.sharding import PartitionSpec as P


def passed_along(block, axis, distance):
    devices = range(lax.axis_size(axis))
    route = [(i - distance, i) for i in devices if i - distance in devices]
    return lax.ppermute(block, axis, route)


def factorize(rows, sketch_cols):
    current = sketch_cols
    summed = None
    for turn in range(2):
        partial_value = jnp.dot(rows, current, preferred_element_type=jnp.float32)
        summed = lax.psum(partial_value, "tensor")
        if turn == 0:
            current = jnp.einsum(
                "td,tr->dr", rows, summed.astype(jnp.bfloat16), preferred_element_type=jnp.float32
            ).astype(jnp.bfloat16)
    gram = jnp.dot(
        summed.T, summed, precision=lax.Precision.HIGHEST, preferred_element_type=jnp.float32
    )
    ridge = 1e-06 * jnp.trace(gram) / gram.shape[0]
    gram = gram + ridge * jnp.eye(gram.shape[0], dtype=jnp.float32)
    lower = jnp.linalg.cholesky(gram)
    basis = lax.linalg.triangular_solve(
        lower, summed, left_side=False, lower=True, transpose_a=True
    ).astype(jnp.bfloat16)
    coeff = jnp.einsum("tr,td->rd", basis, rows, preferred_element_type=jnp.float32).astype(
        jnp.bfloat16
    )
    return (basis, coeff)


def rebuild(basis, coeff):
    return jnp.dot(basis, coeff, preferred_element_type=jnp.float32).astype(jnp.bfloat16)


def shards(section_output, sketch_matrix, boundary_gain, grad_gained):
    rows = section_output[0]
    sketch_cols = sketch_matrix[0]
    scale = boundary_gain[0].astype(jnp.float32)
    upstream = grad_gained[0]
    basis, coeff = factorize(rows, sketch_cols)
    received = passed_along(rebuild(basis, coeff), "section", 1)
    local_grad = jnp.sum(upstream.astype(jnp.float32) * received.astype(jnp.float32), axis=0)
    gain_grad = lax.psum(local_grad, "dp")
    grad_received = (upstream.astype(jnp.float32) * scale[None, :]).astype(jnp.bfloat16)
    back_basis, back_coeff = factorize(grad_received, sketch_cols)
    grad_output = passed_along(rebuild(back_basis, back_coeff), "section", -1)
    return (grad_output[None], gain_grad[None])


def solution(mesh):
    return jax.shard_map(
        shards,
        mesh=mesh,
        in_specs=(
            P("section", "dp", "tensor"),
            P("section", "tensor", None),
            P("section", "tensor"),
            P("section", "dp", "tensor"),
        ),
        out_specs=(P("section", "dp", "tensor"), P("section", "tensor")),
        check_vma=False,
    )
```

profile of v0, /device:TPU:24, one launch (start us, length us, event | category | flops | bytes accessed | tf_op | source)
XLA Modules:
  0.0 183.7 jit_solution(14325029195147675737)
XLA Ops:
  0.7 0.9 mul.46
  1.9 1.4 fusion.17
  3.7 60.1 %all-reduce.1 = (bf16[128,32]{1,0:T(8,128)(2,1)S(1)}, bf16[128,32]{1,0:T(8,128)(2,1)S(1)}) all-reduce(f32[128,32]{1,0:T(8,128)S(1)} %fusion.11, f32[128,32]{1,0:T(8,128)S(1)} %fusion.17), channel_id=1, replica_groups=mesh['dp'=8,'section'=32,'tensor'=4] {'tensor'}, use_global_device_ids=true, to_apply=%region_0.0 | all-reduce | flops 8192 | bytes 49152 | tf_op jit(solution)/shard_map/psum | solution.py:18
  63.8 0.6 fusion.5
  64.4 0.6 fusion.7
  65.1 36.0 %all-reduce = (f32[128,32]{0,1:T(8,128)S(1)}, f32[128,32]{0,1:T(8,128)S(1)}) all-reduce(f32[128,32]{0,1:T(8,128)S(1)} %fusion.5, f32[128,32]{0,1:T(8,128)S(1)} %fusion.7), channel_id=1, replica_groups=mesh['dp'=8,'section'=32,'tensor'=4] {'tensor'}, use_global_device_ids=true, to_apply=%region_1.0 | all-reduce | flops 8192 | bytes 65536 | tf_op jit(solution)/shard_map/psum | solution.py:18
  101.1 0.8 select_reduce_fusion.2
  102.6 2.9 %cholesky.55 = f32[32,32]{1,0:T(8,128)S(1)} custom-call(f32[32,32]{1,0:T(8,128)S(1)} %fusion.33), custom_call_target="Cholesky" | custom-call | tf_op jit(solution)/shard_map/jit(cholesky)/cholesky | solution.py:28
  105.5 0.6 compare_reduce_fusion
  106.2 0.7 fusion.31
  106.8 2.4 %custom-call.7 = f32[1,32,32]{1,2,0:T(8,128)S(1)} custom-call(f32[1,32,32]{2,1,0:T(8,128)S(1)} %fusion.31), custom_call_target="InvertDiagBlocksLowerTriangular" | custom-call | tf_op jit(solution)/shard_map/triangular_solve/custom-call.0 | solution.py:29
  109.5 0.6 convolution_convert_fusion
  110.1 1.9 %collective-permute-start.1 = (bf16[128,4096]{1,0:T(8,128)(2,1)S(1)}, bf16[128,4096]{1,0:T(8,128)(2,1)}, u32[]{:S(2)}, u32[]{:S(2)}) collective-permute-start(bf16[128,4096]{1,0:T(8,128)(2,1)S(1)} %convolution_convert_fusion), channel_id=1, source_target_pairs={{0,4},{4,8},{8,12},{12,16},{16,20},{20,24},{24,28},{28,32},{32,36}... | collective-permute-start | bytes 3145736 | tf_op jit(solution)/shard_map/ppermute | solution.py:10
  112.0 0.8 select_reduce_fusion.3
  113.5 2.9 %cholesky.44 = f32[32,32]{1,0:T(8,128)S(1)} custom-call(f32[32,32]{1,0:T(8,128)S(1)} %fusion.35), custom_call_target="Cholesky" | custom-call | tf_op jit(solution)/shard_map/jit(cholesky)/cholesky | solution.py:28
  116.5 0.6 compare_reduce_fusion.1
  117.1 0.7 fusion.30
  117.8 2.4 %custom-call.6 = f32[1,32,32]{1,2,0:T(8,128)S(1)} custom-call(f32[1,32,32]{2,1,0:T(8,128)S(1)} %fusion.30), custom_call_target="InvertDiagBlocksLowerTriangular" | custom-call | tf_op jit(solution)/shard_map/triangular_solve/custom-call.0 | solution.py:29
  120.4 1.6 convolution_convert_fusion.1
  122.0 5.7 %collective-permute-start = (bf16[128,4096]{1,0:T(8,128)(2,1)}, bf16[128,4096]{1,0:T(8,128)(2,1)}, u32[]{:S(2)}, u32[]{:S(2)}) collective-permute-start(bf16[128,4096]{1,0:T(8,128)(2,1)} %convolution_convert_fusion.1), channel_id=1, source_target_pairs={{4,0},{8,4},{12,8},{16,12},{20,16},{24,20},{28,24},{32,28},{36,32}... | collective-permute-start | bytes 3145736 | tf_op jit(solution)/shard_map/ppermute | solution.py:10
  127.8 0.6 collective-permute-done.1
  128.4 1.5 fusion.3
  129.9 51.5 %psum.39 = f32[1,4096]{1,0:T(1,128)} all-reduce(f32[1,4096]{1,0:T(1,128)S(1)} %bitcast.77), channel_id=1, replica_groups=mesh['dp'=8,'section'=32,'tensor'=4] {'dp'}, use_global_device_ids=true, to_apply=%region_9.12 | all-reduce | flops 4096 | bytes 32768 | tf_op jit(solution)/shard_map/psum | solution.py:50
  181.4 2.3 %copy.21 = bf16[1,128,4096]{2,1,0:T(8,128)(2,1)} copy(bf16[1,128,4096]{2,1,0:T(8,128)(2,1)} %bitcast.8) | data formatting | bytes 2097152
  (18 shorter events, 1.5 us)
Async XLA Ops:
  0.6 1.2 copy-start
  0.6 2.6 %copy-start.2 = (bf16[1,4096,32]{1,2,0:T(8,128)(2,1)S(1)}, bf16[1,4096,32]{1,2,0:T(8,128)(2,1)}, u32[]{:S(2)}) copy-start(bf16[1,4096,32]{1,2,0:T(8,128)(2,1)} %param.8) | copy-start | bytes 786436
  0.7 2.6 %copy-start.1 = (bf16[1,128,4096]{2,1,0:T(8,128)(2,1)S(1)}, bf16[1,128,4096]{2,1,0:T(8,128)(2,1)}, u32[]{:S(2)}) copy-start(bf16[1,128,4096]{2,1,0:T(8,128)(2,1)} %param.10) | copy-start | bytes 3145732
  110.1 18.3 %collective-permute-start.1 = (bf16[128,4096]{1,0:T(8,128)(2,1)S(1)}, bf16[128,4096]{1,0:T(8,128)(2,1)}, u32[]{:S(2)}, u32[]{:S(2)}) collective-permute-start(bf16[128,4096]{1,0:T(8,128)(2,1)S(1)} %convolution_convert_fusion), channel_id=1, source_target_pairs={{0,4},{4,8},{8,12},{12,16},{16,20},{20,24},{24,28},{28,32},{32,36}... | collective-permute-start | bytes 3145736 | tf_op jit(solution)/shard_map/ppermute | solution.py:10
  122.0 59.4 %collective-permute-start = (bf16[128,4096]{1,0:T(8,128)(2,1)}, bf16[128,4096]{1,0:T(8,128)(2,1)}, u32[]{:S(2)}, u32[]{:S(2)}) collective-permute-start(bf16[128,4096]{1,0:T(8,128)(2,1)} %convolution_convert_fusion.1), channel_id=1, source_target_pairs={{4,0},{8,4},{12,8},{16,12},{20,16},{24,20},{28,24},{32,28},{36,32}... | collective-permute-start | bytes 3145736 | tf_op jit(solution)/shard_map/ppermute | solution.py:10
where the time goes:
time: 184 us
  blocking collectives  148 us (80%)
  other arithmetic  15.8 us (9%)
  starting transfers between devices  7.66 us (4%)
  matrix products  7.15 us (4%)
  local copies, waits for them, and re-layouts  2.77 us (2%)
  between operations  2.15 us (1%)
    psum x2, blocking collectives, factorize(): summed = lax.psum(partial_value, 'tensor')  96.1 us
    psum x1, blocking collectives, shards(): gain_grad = lax.psum(local_grad, 'dp')  51.5 us
    ppermute x2, starting transfers between devices, passed_along(): return lax.ppermute(block, axis, route)  7.66 us
    another operation x6, other arithmetic, factorize(): lower = jnp.linalg.cholesky(gram)  7.18 us
    another operation x4, other arithmetic, factorize(): lax.linalg.triangular_solve(lower, summed, left_side=False, lower=True, t...  6.17 us
  transfers between devices with their start and end apart: 2, of which 1 were waited for; matrix products, arithmetic and copies ran while one was open for 6% of the time, Pallas kernels for 0%

commit v1 on v0

v1 whole, which is shorter than its diff:
```python
import jax
import jax.numpy as jnp
from jax import lax
from jax.experimental import pallas as pl
from jax.experimental.pallas import tpu as pltpu
from jax.sharding import PartitionSpec as P


F32 = jnp.float32
BF16 = jnp.bfloat16
HIGHEST = lax.Precision.HIGHEST
RIDGE = 1e-06
SMALL = pltpu.CompilerParams(vmem_limit_bytes=16 * 1024 * 1024)
CONTRACT_LAST = (((1,), (1,)), ((), ()))
CONTRACT_FIRST = (((0,), (0,)), ((), ()))


def indices(shape):
    return (
        lax.broadcasted_iota(jnp.int32, shape, 0),
        lax.broadcasted_iota(jnp.int32, shape, 1),
    )


def packed(gram):
    half = gram.shape[0] // 2
    row, col = indices((half, 2 * half))
    turned = pltpu.roll(gram[half:], half, 1)
    return jnp.where((col < half) & (col >= row), turned, gram[:half])


def unpacked(rows, diagonal):
    half = rows.shape[0]
    row, col = indices((half, 2 * half))
    square = jnp.concatenate([rows, jnp.zeros_like(rows)], axis=0).T
    mirrored, below = square[:half], square[half:]
    first_half = jnp.where(row > col, rows, jnp.where(row < col, mirrored, diagonal))
    top = jnp.where(col < half, first_half, rows)
    shifted = col - half
    turned_rows = pltpu.roll(rows, half, 1)
    turned_mirrored = pltpu.roll(mirrored, half, 1)
    last_half = jnp.where(
        row < shifted, turned_rows, jnp.where(row > shifted, turned_mirrored, diagonal)
    )
    bottom = jnp.where(col < half, below, last_half)
    return jnp.concatenate([top, bottom], axis=0)


def partials_kernel(rows_ref, grad_ref, gain_ref, sketch_ref, out_ref, forward_acc, backward_acc):
    step = pl.program_id(0)
    tokens = rows_ref.shape[0]
    sketch = sketch_ref[...]
    rows = rows_ref[...]
    gained = (grad_ref[...].astype(F32) * gain_ref[...].astype(F32)).astype(BF16)

    def products(block):
        both = jnp.concatenate([block, sketch], axis=0)
        return lax.dot_general(both, block, CONTRACT_LAST, preferred_element_type=F32)

    forward = products(rows)
    backward = products(gained)

    @pl.when(step == 0)
    def _():
        forward_acc[...] = forward
        backward_acc[...] = backward

    @pl.when(step > 0)
    def _():
        forward_acc[...] += forward
        backward_acc[...] += backward

    @pl.when(step == pl.num_programs(0) - 1)
    def _():
        half = tokens // 2
        rank = sketch.shape[0]
        row, col = indices((tokens, tokens))
        diagonals = []
        for turn, acc in enumerate((forward_acc, backward_acc)):
            gram = acc[:tokens]
            out_ref[turn * half : (turn + 1) * half] = packed(gram).astype(BF16)
            at = 2 * half + turn * rank
            out_ref[at : at + rank] = acc[tokens:].astype(BF16)
            diagonal = jnp.sum(jnp.where(row == col, gram, 0.0), axis=0, keepdims=True)
            high = diagonal.astype(BF16).astype(F32)
            diagonals += [high, diagonal - high]
        rest = jnp.zeros((out_ref.shape[0] - 2 * half - 2 * rank - 4, tokens), F32)
        tail = jnp.concatenate(diagonals + [rest], axis=0)
        out_ref[2 * half + 2 * rank :] = tail.astype(BF16)


def orthonormal(gram, first):
    rank, _ = first.shape
    sketch = lax.dot_general(
        first, gram, (((1,), (0,)), ((), ())), precision=HIGHEST, preferred_element_type=F32
    )
    small = lax.dot_general(
        sketch, sketch, CONTRACT_LAST, precision=HIGHEST, preferred_element_type=F32
    )
    row, col = indices((rank, rank))
    trace = jnp.sum(jnp.where(row == col, small, 0.0), keepdims=True)
    small = small + jnp.where(row == col, trace * (RIDGE / rank), 0.0)
    return sketch, small


def eliminate(pairs):
    rank = pairs[0][0].shape[0]
    states = [list(pair) for pair in pairs]
    done = [[] for _ in pairs]
    for k in range(rank):
        for state, finished in zip(states, done):
            sketch, small = state
            pivot = small[k : k + 1, k : k + 1]
            scale = lax.rsqrt(pivot)
            scale = scale * (1.5 - 0.5 * pivot * scale * scale)
            sketch_row = sketch[k : k + 1] * scale
            finished.append(sketch_row)
            if k + 1 < rank:
                small_row = small[k : k + 1] * scale
                column = small[:, k : k + 1] * scale
                state[0] = sketch - column * sketch_row
                state[1] = small - column * small_row
    return [jnp.concatenate(finished, axis=0) for finished in done]


def factor_kernel(
    gathered_ref, rows_hbm, next_hbm, local_ref, forward_ref, backward_ref, rows_ref, next_ref, sems
):
    copies = [
        pltpu.make_async_copy(rows_hbm, rows_ref, sems.at[0]),
        pltpu.make_async_copy(next_hbm, next_ref, sems.at[1]),
    ]
    for copy in copies:
        copy.start()
    tokens, width = rows_ref.shape
    rank = backward_ref.shape[0]
    half = tokens // 2
    total = gathered_ref[0].astype(F32)
    for member in range(1, gathered_ref.shape[0]):
        total = total + gathered_ref[member].astype(F32)
    pairs = []
    for turn in range(2):
        at = 2 * half + turn * rank
        mark = 2 * half + 2 * rank + 2 * turn
        diagonal = total[mark : mark + 1] + total[mark + 1 : mark + 2]
        gram = unpacked(total[turn * half : (turn + 1) * half], diagonal)
        pairs.append(orthonormal(gram, total[at : at + rank]))
    forward, backward = (basis.astype(BF16) for basis in eliminate(pairs))
    forward_ref[...] = forward
    backward_ref[...] = backward
    for copy in copies:
        copy.wait()
    chunk = 1024
    for start in range(0, width, chunk):
        coeff = jnp.dot(
            forward, rows_ref[:, start : start + chunk], preferred_element_type=F32
        ).astype(BF16)
        other = jnp.dot(forward, next_ref[:, start : start + chunk], preferred_element_type=F32)
        summed = jnp.sum(coeff.astype(F32) * other, axis=0, keepdims=True)
        for lane in range(0, chunk, 128):
            at = (start + lane) // 128
            local_ref[at : at + 1] = summed[:, lane : lane + 128]


def coeff_kernel(basis_ref, grad_ref, gain_ref, out_ref):
    width = grad_ref.shape[1]
    basis = basis_ref[...]
    gained = (grad_ref[...].astype(F32) * gain_ref[...].astype(F32)).astype(BF16)
    out_ref[:, :width] = jnp.dot(basis, gained, preferred_element_type=F32).astype(BF16)
    out_ref[:, width:] = basis


def rebuild_kernel(coeff_ref, basis_ref, out_ref):
    out_ref[...] = lax.dot_general(
        basis_ref[...], coeff_ref[...], CONTRACT_FIRST, preferred_element_type=F32
    ).astype(BF16)


def partials(rows, grad, gain, sketch_rows):
    tokens, width = rows.shape
    rank = sketch_rows.shape[0]
    chunk = 1024
    return pl.pallas_call(
        partials_kernel,
        out_shape=jax.ShapeDtypeStruct((tokens + 2 * rank + 8, tokens), BF16),
        grid=(width // chunk,),
        in_specs=[
            pl.BlockSpec((tokens, chunk), lambda i: (0, i)),
            pl.BlockSpec((tokens, chunk), lambda i: (0, i)),
            pl.BlockSpec((1, chunk), lambda i: (0, i)),
            pl.BlockSpec((rank, chunk), lambda i: (0, i)),
        ],
        out_specs=pl.BlockSpec((tokens + 2 * rank + 8, tokens), lambda i: (0, 0)),
        scratch_shapes=[
            pltpu.VMEM((tokens + rank, tokens), F32),
            pltpu.VMEM((tokens + rank, tokens), F32),
        ],
        name="partials",
    )(rows, grad, gain, sketch_rows)


def factors(gathered, rows, next_grad, rank):
    tokens, width = rows.shape
    vmem = pl.BlockSpec(memory_space=pltpu.VMEM)
    anywhere = pl.BlockSpec(memory_space=pl.ANY)
    basis = jax.ShapeDtypeStruct((rank, tokens), BF16)
    return pl.pallas_call(
        factor_kernel,
        out_shape=(jax.ShapeDtypeStruct((width // 128, 128), F32), basis, basis),
        in_specs=[vmem, anywhere, anywhere],
        out_specs=(vmem, vmem, vmem),
        scratch_shapes=[
            pltpu.VMEM((tokens, width), BF16),
            pltpu.VMEM((tokens, width), BF16),
            pltpu.SemaphoreType.DMA((2,)),
        ],
        compiler_params=SMALL,
        name="factors",
    )(gathered, rows, next_grad)


def coefficients(basis, grad, gain):
    rank, tokens = basis.shape
    width = grad.shape[1]
    vmem = pl.BlockSpec(memory_space=pltpu.VMEM)
    return pl.pallas_call(
        coeff_kernel,
        out_shape=jax.ShapeDtypeStruct((rank, width + tokens), BF16),
        in_specs=[vmem, vmem, vmem],
        out_specs=vmem,
        compiler_params=SMALL,
        name="coefficients",
    )(basis, grad, gain)


def rebuild(both, tokens):
    rank = both.shape[0]
    width = both.shape[1] - tokens
    chunk = 1024
    return pl.pallas_call(
        rebuild_kernel,
        out_shape=jax.ShapeDtypeStruct((tokens, width), BF16),
        grid=(width // chunk,),
        in_specs=[
            pl.BlockSpec((rank, chunk), lambda i: (0, i)),
            pl.BlockSpec((rank, tokens), lambda i: (0, width // tokens)),
        ],
        out_specs=pl.BlockSpec((tokens, chunk), lambda i: (0, i)),
        compiler_params=SMALL,
        name="rebuild",
    )(both, both)


def along_section(block, distance):
    devices = range(lax.axis_size("section"))
    route = [(i, i + distance) for i in devices if i + distance in devices]
    return lax.ppermute(block, "section", route)


def exchange(block, bit):
    return lax.ppermute(block, "dp", [(i, i ^ bit) for i in range(lax.axis_size("dp"))])


def exchange_along(block, bit):
    sections, members = lax.axis_size("section"), lax.axis_size("dp")
    route = [
        (i * sections + s, (i ^ bit) * sections + s + 1)
        for i in range(members)
        for s in range(sections - 1)
    ]
    return lax.ppermute(block, ("dp", "section"), route)


def shards(section_output, sketch_matrix, boundary_gain, grad_gained):
    rows = section_output[0]
    sketch_rows = sketch_matrix[0].T
    grad = grad_gained[0]
    tokens = rows.shape[0]
    next_grad = along_section(grad, -1)
    mine = partials(rows, grad, boundary_gain, sketch_rows)
    gathered = lax.all_gather(mine, "tensor")
    local, _, backward = factors(gathered, rows, next_grad, sketch_rows.shape[0])
    far = exchange(local, 4)
    both = coefficients(backward, grad, boundary_gain)
    both = along_section(both, -1)
    summed = local + far
    middle = exchange(summed, 2)
    summed = summed + middle
    own = exchange_along(summed, 0)
    near = exchange_along(summed, 1)
    gain_grad = own + near
    grad_output = rebuild(both, tokens)
    return grad_output[None], gain_grad.reshape(1, -1)


def solution(mesh):
    return jax.shard_map(
        shards,
        mesh=mesh,
        in_specs=(
            P("section", "dp", "tensor"),
            P("section", "tensor", None),
            P("section", "tensor"),
            P("section", "dp", "tensor"),
        ),
        out_specs=(P("section", "dp", "tensor"), P("section", "tensor")),
        check_vma=False,
    )
```

time: 184 us -> 94.5 us (0.51)
  blocking collectives: 148 us -> 47 us
  waiting for transfers between devices: 0.61 us -> 18.1 us
  other arithmetic: 15.8 us -> 0.62 us
  Pallas kernels: 0 us -> 11.1 us
  starting transfers between devices: 7.66 us -> 16.6 us
  matrix products: 7.15 us -> 0 us
  local copies, waits for them, and re-layouts: 2.77 us -> 0.02 us
    psum x3 -> x0, blocking collectives: 148 us -> none  [the longest x2 96.1 us: factorize(): summed = lax.psum(partial_value, 'tensor')]
    all_gather x0 -> x1, blocking collectives: none -> 47 us  [shards(): gathered = lax.all_gather(mine, 'tensor')]
    ppermute x2 -> x6, waiting for transfers between devices: 0.61 us -> 18.1 us  [the longest x2 12.2 us: exchange(): lax.ppermute(block, 'dp', [(i, i ^ bit) for i in range(lax.axis_size('dp'...]
    another operation x10 -> x0, other arithmetic: 13.4 us -> none  [the longest x6 7.18 us: factorize(): lower = jnp.linalg.cholesky(gram)]
    pallas_call x0 -> x4, Pallas kernels: none -> 11.1 us  [the longest x1 4.48 us: factors(): pl.pallas_call(factor_kernel, out_shape=(jax.ShapeDtypeStruct((width // 1...]
    ppermute x2 -> x6, starting transfers between devices: 7.66 us -> 16.6 us  [the longest x2 8.31 us: along_section(): return lax.ppermute(block, 'section', route)]
    dot_general x8 -> x0, matrix products: 6.67 us -> none  [the longest x4 3 us: factorize(): partial_value = jnp.dot(rows, current, preferred_element_type=jnp.float32)]
    unnamed x7 -> x6, local copies, waits for them, and re-layouts: 2.63 us -> 0.02 us
  transfers between devices with their start and end apart: 2 -> 6, of which waited for: 1 -> 4; matrix products, arithmetic and copies ran while one was open for 6% -> 1% of each run, Pallas kernels for 0% -> 4%
where the time goes in v1:
time: 94.5 us; the launch traced here: 94.2 us
  blocking collectives  47 us (50%)
  waiting for transfers between devices  18.1 us (19%)
  starting transfers between devices  16.6 us (18%)
  Pallas kernels  11.1 us (12%)
    all_gather x1, blocking collectives, shards(): gathered = lax.all_gather(mine, 'tensor')  47 us
    ppermute x2, waiting for transfers between devices, exchange(): lax.ppermute(block, 'dp', [(i, i ^ bit) for i in range(lax.axis_size('dp'...  12.2 us
    ppermute x2, starting transfers between devices, along_section(): return lax.ppermute(block, 'section', route)  8.31 us
    ppermute x2, waiting for transfers between devices, exchange_along(): return lax.ppermute(block, ('dp', 'section'), route)  5.89 us
    pallas_call x1, Pallas kernels, factors(): pl.pallas_call(factor_kernel, out_shape=(jax.ShapeDtypeStruct((width // 1...  4.48 us
    ppermute x2, starting transfers between devices, exchange_along(): return lax.ppermute(block, ('dp', 'section'), route)  4.45 us
    pallas_call x1, Pallas kernels, partials(): pl.pallas_call(partials_kernel, out_shape=jax.ShapeDtypeStruct((tokens +...  4.02 us
    ppermute x2, starting transfers between devices, exchange(): lax.ppermute(block, 'dp', [(i, i ^ bit) for i in range(lax.axis_size('dp'...  3.83 us
  transfers between devices with their start and end apart: 6, of which 4 were waited for; matrix products, arithmetic and copies ran while one was open for 1% of the time, Pallas kernels for 4%

profile of v1, /device:TPU:24, one launch (start us, length us, event | category | flops | bytes accessed | tf_op | source)
XLA Modules:
  0.0 94.2 jit_solution(3837373315640607325)
XLA Ops:
  0.6 4.3 %collective-permute-start = (bf16[128,4096]{1,0:T(8,128)(2,1)}, bf16[128,4096]{1,0:T(8,128)(2,1)S(1)}, u32[]{:S(2)}, u32[]{:S(2)}) collective-permute-start(bf16[128,4096]{1,0:T(8,128)(2,1)} %bitcast.10), channel_id=1, source_target_pairs={{4,0},{8,4},{12,8},{16,12},{20,16},{24,20},{28,24},{32,28},{36,32}... | collective-permute-start | bytes 3145736 | tf_op jit(solution)/shard_map/ppermute | solution.py:257
  4.9 0.0 copy-start
  4.9 4.0 %partials.1 = bf16[200,128]{1,0:T(8,128)(2,1)} custom-call(bf16[128,4096]{1,0:T(8,128)(2,1)} %bitcast.8, bf16[128,4096]{1,0:T(8,128)(2,1)} %bitcast.11, bf16[1,4096]{1,0:T(2,128)(2,1)} %gain_ref.3, bf16[32,4096]{1,0:T(8,128)(2,1)} %bitcast.15), custom_call_target="tpu_custom_call" | custom-call | tf_op jit(solution)/shard_map/partials/pallas_call | solution.py:183
  9.0 47.0 %all-gather = bf16[800,128]{1,0:T(8,128)(2,1)S(1)} all-gather(bf16[200,128]{1,0:T(8,128)(2,1)} %partials.1), channel_id=2, replica_groups=mesh['dp'=8,'section'=32,'tensor'=4] {'tensor'}, dimensions={0}, use_global_device_ids=true | all-gather | bytes 256000 | tf_op jit(solution)/shard_map/all_gather | solution.py:281
  56.0 0.0 collective-permute-done.next_hbm
  56.0 0.0 copy-done
  56.0 0.0 copy-start.1
  56.0 0.0 copy-start.2
  56.0 4.5 %factors.1 = (f32[32,128]{1,0:T(8,128)S(1)}, bf16[32,128]{1,0:T(8,128)(2,1)}, bf16[32,128]{1,0:T(8,128)(2,1)S(1)}) custom-call(bf16[4,200,128]{2,1,0:T(8,128)(2,1)S(1)} %bitcast.13, bf16[128,4096]{1,0:T(8,128)(2,1)S(1)} %bitcast.9, bf16[128,4096]{1,0:T(8,128)(2,1)S(1)} %collective-permute-done.next_hbm), custom_call_target="tpu_custom_call" | custom-call | tf_op jit(solution)/shard_map/factors/pallas_call | solution.py:207
  60.5 0.0 copy-done.1
  60.5 0.0 copy-done.2
  60.5 0.3 coefficients.1
  60.8 4.0 %collective-permute-start.1 = (bf16[32,4224]{1,0:T(8,128)(2,1)S(1)}, bf16[32,4224]{1,0:T(8,128)(2,1)S(1)}, u32[]{:S(2)}, u32[]{:S(2)}) collective-permute-start(bf16[32,4224]{1,0:T(8,128)(2,1)S(1)} %coefficients.1), channel_id=1, source_target_pairs={{4,0},{8,4},{12,8},{16,12},{20,16},{24,20},{28,24},{32,28},{36,32}... | collective-permute-start | bytes 811016 | tf_op jit(solution)/shard_map/ppermute | solution.py:257
  64.8 1.9 %collective-permute-start.2 = (f32[32,128]{1,0:T(8,128)S(1)}, f32[32,128]{1,0:T(8,128)S(1)}, u32[]{:S(2)}, u32[]{:S(2)}) collective-permute-start(f32[32,128]{1,0:T(8,128)S(1)} %get-tuple-element.5), channel_id=1, source_target_pairs={{0,512},{128,640},{256,768},{384,896},{512,0},{640,128},{768,256},... | collective-permute-start | bytes 49160 | tf_op jit(solution)/shard_map/ppermute | solution.py:261
  66.8 7.6 %collective-permute-done.2 = f32[32,128]{1,0:T(8,128)S(1)} collective-permute-done((f32[32,128]{1,0:T(8,128)S(1)}, f32[32,128]{1,0:T(8,128)S(1)}, u32[]{:S(2)}, u32[]{:S(2)}) %collective-permute-start.2) | collective-permute-done | bytes 16416 | tf_op jit(solution)/shard_map/ppermute | solution.py:261
  74.4 1.9 %collective-permute-start.3 = (f32[32,128]{1,0:T(8,128)S(1)}, f32[32,128]{1,0:T(8,128)S(1)}, u32[]{:S(2)}, u32[]{:S(2)}) collective-permute-start(f32[32,128]{1,0:T(8,128)S(1)} %add.9), channel_id=1, source_target_pairs={{0,256},{128,384},{256,0},{384,128},{512,768},{640,896},{768,512},... | collective-permute-start | bytes 49160 | tf_op jit(solution)/shard_map/ppermute | solution.py:261
  76.3 4.6 %collective-permute-done.3 = f32[32,128]{1,0:T(8,128)S(1)} collective-permute-done((f32[32,128]{1,0:T(8,128)S(1)}, f32[32,128]{1,0:T(8,128)S(1)}, u32[]{:S(2)}, u32[]{:S(2)}) %collective-permute-start.3) | collective-permute-done | bytes 16416 | tf_op jit(solution)/shard_map/ppermute | solution.py:261
  80.9 1.9 %collective-permute-start.5 = (f32[32,128]{1,0:T(8,128)S(1)}, f32[32,128]{1,0:T(8,128)S(1)}, u32[]{:S(2)}, u32[]{:S(2)}) collective-permute-start(f32[32,128]{1,0:T(8,128)S(1)} %add.10), channel_id=1, source_target_pairs={{0,132},{4,136},{8,140},{12,144},{16,148},{20,152},{24,156},{28,16... | collective-permute-start | bytes 49160 | tf_op jit(solution)/shard_map/ppermute | solution.py:271
  82.8 2.5 %collective-permute-start.4 = (f32[32,128]{1,0:T(8,128)S(1)}, f32[32,128]{1,0:T(8,128)S(1)}, u32[]{:S(2)}, u32[]{:S(2)}) collective-permute-start(f32[32,128]{1,0:T(8,128)S(1)} %add.10), channel_id=1, source_target_pairs={{0,4},{4,8},{8,12},{12,16},{16,20},{20,24},{24,28},{28,32},{32,36}... | collective-permute-start | bytes 49160 | tf_op jit(solution)/shard_map/ppermute | solution.py:271
  85.4 3.6 %collective-permute-done.5 = f32[32,128]{1,0:T(8,128)S(1)} collective-permute-done((f32[32,128]{1,0:T(8,128)S(1)}, f32[32,128]{1,0:T(8,128)S(1)}, u32[]{:S(2)}, u32[]{:S(2)}) %collective-permute-start.5) | collective-permute-done | bytes 16416 | tf_op jit(solution)/shard_map/ppermute | solution.py:271
  89.0 2.3 %collective-permute-done.4 = f32[32,128]{1,0:T(8,128)S(1)} collective-permute-done((f32[32,128]{1,0:T(8,128)S(1)}, f32[32,128]{1,0:T(8,128)S(1)}, u32[]{:S(2)}, u32[]{:S(2)}) %collective-permute-start.4) | collective-permute-done | bytes 16416 | tf_op jit(solution)/shard_map/ppermute | solution.py:271
  91.3 0.6 add.11
  91.9 0.0 collective-permute-done.1.coeff_ref.basis_ref
  91.9 2.3 %rebuild.1 = bf16[128,4096]{1,0:T(8,128)(2,1)} custom-call(bf16[32,4224]{1,0:T(8,128)(2,1)S(1)} %collective-permute-done.1.coeff_ref.basis_ref, bf16[32,4224]{1,0:T(8,128)(2,1)S(1)} %collective-permute-done.1.coeff_ref.basis_ref), custom_call_target="tpu_custom_call" | custom-call | tf_op jit(solution)/shard_map/rebuild/pallas_call | solution.py:240
  (2 shorter events, 0.0 us)
Async XLA Ops:
  0.6 55.3 %collective-permute-start = (bf16[128,4096]{1,0:T(8,128)(2,1)}, bf16[128,4096]{1,0:T(8,128)(2,1)S(1)}, u32[]{:S(2)}, u32[]{:S(2)}) collective-permute-start(bf16[128,4096]{1,0:T(8,128)(2,1)} %bitcast.10), channel_id=1, source_target_pairs={{4,0},{8,4},{12,8},{16,12},{20,16},{24,20},{28,24},{32,28},{36,32}... | collective-permute-start | bytes 3145736 | tf_op jit(solution)/shard_map/ppermute | solution.py:257
  4.9 51.0 %copy-start = (bf16[1,128,4096]{2,1,0:T(8,128)(2,1)S(1)}, bf16[1,128,4096]{2,1,0:T(8,128)(2,1)}, u32[]{:S(2)}) copy-start(bf16[1,128,4096]{2,1,0:T(8,128)(2,1)} %param.4) | copy-start | bytes 3145732
  56.0 4.5 %copy-start.1 = (bf16[1,128,4096]{2,1,0:T(8,128)(2,1)S(1)}, bf16[1,128,4096]{2,1,0:T(8,128)(2,1)}, u32[]{:S(2)}) copy-start(bf16[1,128,4096]{2,1,0:T(8,128)(2,1)} %param.7) | copy-start | bytes 3145732
  56.0 4.5 %copy-start.2 = (bf16[1,4096]{1,0:T(2,128)(2,1)S(1)}, bf16[1,4096]{1,0:T(2,128)(2,1)}, u32[]{:S(2)}) copy-start(bf16[1,4096]{1,0:T(2,128)(2,1)} %gain_ref.3) | copy-start | bytes 24580
  60.8 31.1 %collective-permute-start.1 = (bf16[32,4224]{1,0:T(8,128)(2,1)S(1)}, bf16[32,4224]{1,0:T(8,128)(2,1)S(1)}, u32[]{:S(2)}, u32[]{:S(2)}) collective-permute-start(bf16[32,4224]{1,0:T(8,128)(2,1)S(1)} %coefficients.1), channel_id=1, source_target_pairs={{4,0},{8,4},{12,8},{16,12},{20,16},{24,20},{28,24},{32,28},{36,32}... | collective-permute-start | bytes 811016 | tf_op jit(solution)/shard_map/ppermute | solution.py:257
  64.8 9.5 %collective-permute-start.2 = (f32[32,128]{1,0:T(8,128)S(1)}, f32[32,128]{1,0:T(8,128)S(1)}, u32[]{:S(2)}, u32[]{:S(2)}) collective-permute-start(f32[32,128]{1,0:T(8,128)S(1)} %get-tuple-element.5), channel_id=1, source_target_pairs={{0,512},{128,640},{256,768},{384,896},{512,0},{640,128},{768,256},... | collective-permute-start | bytes 49160 | tf_op jit(solution)/shard_map/ppermute | solution.py:261
  74.4 6.5 %collective-permute-start.3 = (f32[32,128]{1,0:T(8,128)S(1)}, f32[32,128]{1,0:T(8,128)S(1)}, u32[]{:S(2)}, u32[]{:S(2)}) collective-permute-start(f32[32,128]{1,0:T(8,128)S(1)} %add.9), channel_id=1, source_target_pairs={{0,256},{128,384},{256,0},{384,128},{512,768},{640,896},{768,512},... | collective-permute-start | bytes 49160 | tf_op jit(solution)/shard_map/ppermute | solution.py:261
  80.9 8.1 %collective-permute-start.5 = (f32[32,128]{1,0:T(8,128)S(1)}, f32[32,128]{1,0:T(8,128)S(1)}, u32[]{:S(2)}, u32[]{:S(2)}) collective-permute-start(f32[32,128]{1,0:T(8,128)S(1)} %add.10), channel_id=1, source_target_pairs={{0,132},{4,136},{8,140},{12,144},{16,148},{20,152},{24,156},{28,16... | collective-permute-start | bytes 49160 | tf_op jit(solution)/shard_map/ppermute | solution.py:271
  82.8 8.4 %collective-permute-start.4 = (f32[32,128]{1,0:T(8,128)S(1)}, f32[32,128]{1,0:T(8,128)S(1)}, u32[]{:S(2)}, u32[]{:S(2)}) collective-permute-start(f32[32,128]{1,0:T(8,128)S(1)} %add.10), channel_id=1, source_target_pairs={{0,4},{4,8},{8,12},{12,16},{16,20},{20,24},{24,28},{28,32},{32,36}... | collective-permute-start | bytes 49160 | tf_op jit(solution)/shard_map/ppermute | solution.py:271

commit v2 on v1

--- a/solution.py
+++ b/solution.py
@@ -10,9 +10,10 @@
 BF16 = jnp.bfloat16
 HIGHEST = lax.Precision.HIGHEST
 RIDGE = 1e-06
+CHUNKS = 4
+BLOCK = 4
 SMALL = pltpu.CompilerParams(vmem_limit_bytes=16 * 1024 * 1024)
 CONTRACT_LAST = (((1,), (1,)), ((), ()))
-CONTRACT_FIRST = (((0,), (0,)), ((), ()))
 
 
 def indices(shape):
@@ -46,47 +47,59 @@
     return jnp.concatenate([top, bottom], axis=0)
 
 
-def partials_kernel(rows_ref, grad_ref, gain_ref, sketch_ref, out_ref, forward_acc, backward_acc):
-    step = pl.program_id(0)
-    tokens = rows_ref.shape[0]
-    sketch = sketch_ref[...]
-    rows = rows_ref[...]
-    gained = (grad_ref[...].astype(F32) * gain_ref[...].astype(F32)).astype(BF16)
-
-    def products(block):
-        both = jnp.concatenate([block, sketch], axis=0)
-        return lax.dot_general(both, block, CONTRACT_LAST, preferred_element_type=F32)
-
-    forward = products(rows)
-    backward = products(gained)
-
-    @pl.when(step == 0)
-    def _():
-        forward_acc[...] = forward
-        backward_acc[...] = backward
-
-    @pl.when(step > 0)
-    def _():
-        forward_acc[...] += forward
-        backward_acc[...] += backward
-
-    @pl.when(step == pl.num_programs(0) - 1)
-    def _():
-        half = tokens // 2
-        rank = sketch.shape[0]
-        row, col = indices((tokens, tokens))
-        diagonals = []
-        for turn, acc in enumerate((forward_acc, backward_acc)):
-            gram = acc[:tokens]
-            out_ref[turn * half : (turn + 1) * half] = packed(gram).astype(BF16)
-            at = 2 * half + turn * rank
-            out_ref[at : at + rank] = acc[tokens:].astype(BF16)
-            diagonal = jnp.sum(jnp.where(row == col, gram, 0.0), axis=0, keepdims=True)
-            high = diagonal.astype(BF16).astype(F32)
-            diagonals += [high, diagonal - high]
-        rest = jnp.zeros((out_ref.shape[0] - 2 * half - 2 * rank - 4, tokens), F32)
-        tail = jnp.concatenate(diagonals + [rest], axis=0)
-        out_ref[2 * half + 2 * rank :] = tail.astype(BF16)
+def partials_kernel(
+    rows_hbm, grad_hbm, gain_hbm, sketch_hbm, out_ref, rows_ref, grad_ref, gain_ref, sketch_ref, sems
+):
+    tokens, width = rows_ref.shape
+    rank = sketch_ref.shape[0]
+    chunk = width // CHUNKS
+    small = [
+        pltpu.make_async_copy(sketch_hbm, sketch_ref, sems.at[2 * CHUNKS]),
+        pltpu.make_async_copy(gain_hbm, gain_ref, sems.at[2 * CHUNKS + 1]),
+    ]
+    large = []
+    for turn, (source, target) in enumerate(((rows_hbm, rows_ref), (grad_hbm, grad_ref))):
+        for i in range(CHUNKS):
+            at = pl.ds(i * chunk, chunk)
+            large.append(
+                pltpu.make_async_copy(
+                    source.at[:, at], target.at[:, at], sems.at[turn * CHUNKS + i]
+                )
+            )
+    for copy in small + large:
+        copy.start()
+    for copy in small:
+        copy.wait()
+    totals = []
+    for turn in range(2):
+        total = None
+        for i in range(CHUNKS):
+            at = slice(i * chunk, (i + 1) * chunk)
+            large[turn * CHUNKS + i].wait()
+            if turn == 0:
+                block = rows_ref[:, at]
+            else:
+                block = grad_ref[:, at].astype(F32) * gain_ref[:, at].astype(F32)
+                block = block.astype(BF16)
+            product = [
+                lax.dot_general(left, block, CONTRACT_LAST, preferred_element_type=F32)
+                for left in (block, sketch_ref[:, at])
+            ]
+            total = product if total is None else [a + b for a, b in zip(total, product)]
+        totals.append(total)
+    half = tokens // 2
+    row, col = indices((tokens, tokens))
+    diagonals = []
+    for turn, (gram, first) in enumerate(totals):
+        out_ref[turn * half : (turn + 1) * half] = packed(gram).astype(BF16)
+        at = 2 * half + turn * rank
+        out_ref[at : at + rank] = first.astype(BF16)
+        diagonal = jnp.sum(jnp.where(row == col, gram, 0.0), axis=0, keepdims=True)
+        high = diagonal.astype(BF16).astype(F32)
+        diagonals += [high, diagonal - high]
+    rest = jnp.zeros((out_ref.shape[0] - 2 * half - 2 * rank - 4, tokens), F32)
+    tail = jnp.concatenate(diagonals + [rest], axis=0)
+    out_ref[2 * half + 2 * rank :] = tail.astype(BF16)
 
 
 def orthonormal(gram, first):
@@ -104,22 +117,40 @@
 
 
 def eliminate(pairs):
-    rank = pairs[0][0].shape[0]
-    states = [list(pair) for pair in pairs]
+    rank, tokens = pairs[0][0].shape
+    states = [
+        jnp.concatenate(
+            [sketch, small, jnp.zeros((rank, tokens - rank), F32)], axis=1
+        )
+        for sketch, small in pairs
+    ]
     done = [[] for _ in pairs]
-    for k in range(rank):
-        for state, finished in zip(states, done):
-            sketch, small = state
-            pivot = small[k : k + 1, k : k + 1]
-            scale = lax.rsqrt(pivot)
-            scale = scale * (1.5 - 0.5 * pivot * scale * scale)
-            sketch_row = sketch[k : k + 1] * scale
-            finished.append(sketch_row)
-            if k + 1 < rank:
-                small_row = small[k : k + 1] * scale
-                column = small[:, k : k + 1] * scale
-                state[0] = sketch - column * sketch_row
-                state[1] = small - column * small_row
+    for start in range(0, rank, BLOCK):
+        spread = [
+            [
+                jnp.broadcast_to(
+                    state[:, tokens + k : tokens + k + 1], (rank, tokens)
+                )
+                for k in range(start, start + BLOCK)
+            ]
+            for state in states
+        ]
+        for j in range(BLOCK):
+            k = start + j
+            for n, columns in enumerate(spread):
+                column = columns[j]
+                pivot = column[k : k + 1]
+                inverse = 1.0 / pivot
+                inverse2 = jnp.concatenate([inverse, inverse], axis=1)
+                row = states[n][k : k + 1]
+                scale = lax.rsqrt(pivot)
+                scale = scale * (1.5 - 0.5 * pivot * scale * scale)
+                done[n].append(row[:, :tokens] * scale)
+                column2 = jnp.concatenate([column, column], axis=1)
+                states[n] = states[n] - column2 * (row * inverse2)
+                for m in range(j + 1, BLOCK):
+                    other = column[start + m : start + m + 1] * inverse
+                    columns[m] = columns[m] - column * other
     return [jnp.concatenate(finished, axis=0) for finished in done]
 
 
@@ -170,30 +201,40 @@
     out_ref[:, width:] = basis
 
 
-def rebuild_kernel(coeff_ref, basis_ref, out_ref):
-    out_ref[...] = lax.dot_general(
-        basis_ref[...], coeff_ref[...], CONTRACT_FIRST, preferred_element_type=F32
-    ).astype(BF16)
+def rebuild_kernel(both_ref, out_hbm, out_ref, sems):
+    _, width = out_ref.shape
+    basis = both_ref[:, width:].T
+    chunk = width // CHUNKS
+    copies = []
+    for i in range(CHUNKS):
+        at = i * chunk
+        out_ref[:, at : at + chunk] = jnp.dot(
+            basis, both_ref[:, at : at + chunk], preferred_element_type=F32
+        ).astype(BF16)
+        window = pl.ds(at, chunk)
+        copies.append(
+            pltpu.make_async_copy(out_ref.at[:, window], out_hbm.at[:, window], sems.at[i])
+        )
+        copies[-1].start()
+    for copy in copies:
+        copy.wait()
 
 
 def partials(rows, grad, gain, sketch_rows):
     tokens, width = rows.shape
     rank = sketch_rows.shape[0]
-    chunk = 1024
+    anywhere = pl.BlockSpec(memory_space=pl.ANY)
     return pl.pallas_call(
         partials_kernel,
         out_shape=jax.ShapeDtypeStruct((tokens + 2 * rank + 8, tokens), BF16),
-        grid=(width // chunk,),
-        in_specs=[
-            pl.BlockSpec((tokens, chunk), lambda i: (0, i)),
-            pl.BlockSpec((tokens, chunk), lambda i: (0, i)),
-            pl.BlockSpec((1, chunk), lambda i: (0, i)),
-            pl.BlockSpec((rank, chunk), lambda i: (0, i)),
-        ],
-        out_specs=pl.BlockSpec((tokens + 2 * rank + 8, tokens), lambda i: (0, 0)),
+        in_specs=[anywhere] * 4,
+        out_specs=pl.BlockSpec(memory_space=pltpu.VMEM),
         scratch_shapes=[
-            pltpu.VMEM((tokens + rank, tokens), F32),
-            pltpu.VMEM((tokens + rank, tokens), F32),
+            pltpu.VMEM((tokens, width), BF16),
+            pltpu.VMEM((tokens, width), BF16),
+            pltpu.VMEM((1, width), BF16),
+            pltpu.VMEM((rank, width), BF16),
+            pltpu.SemaphoreType.DMA((2 * CHUNKS + 2,)),
         ],
         name="partials",
     )(rows, grad, gain, sketch_rows)
@@ -234,21 +275,19 @@
 
 
 def rebuild(both, tokens):
-    rank = both.shape[0]
     width = both.shape[1] - tokens
-    chunk = 1024
     return pl.pallas_call(
         rebuild_kernel,
         out_shape=jax.ShapeDtypeStruct((tokens, width), BF16),
-        grid=(width // chunk,),
-        in_specs=[
-            pl.BlockSpec((rank, chunk), lambda i: (0, i)),
-            pl.BlockSpec((rank, tokens), lambda i: (0, width // tokens)),
+        in_specs=[pl.BlockSpec(memory_space=pltpu.VMEM)],
+        out_specs=pl.BlockSpec(memory_space=pl.ANY),
+        scratch_shapes=[
+            pltpu.VMEM((tokens, width), BF16),
+            pltpu.SemaphoreType.DMA((CHUNKS,)),
         ],
-        out_specs=pl.BlockSpec((tokens, chunk), lambda i: (0, i)),
         compiler_params=SMALL,
         name="rebuild",
-    )(both, both)
+    )(both)
 
 
 def along_section(block, distance):

time: 94.5 us -> 91 us (0.963)
  Pallas kernels: 11.1 us -> 7.87 us
  waiting for transfers between devices: 18.1 us -> 17 us
    pallas_call x1, Pallas kernels: 4.48 us -> 2.67 us  [factors(): pl.pallas_call(factor_kernel, out_shape=(jax.ShapeDtypeStruct((width // 1...]
    pallas_call x1, Pallas kernels: 2.3 us -> 1.25 us  [rebuild(): pl.pallas_call(rebuild_kernel, out_shape=jax.ShapeDtypeStruct((tokens, wi...]
    ppermute x2, waiting for transfers between devices: 5.89 us -> 4.93 us  [exchange_along(): return lax.ppermute(block, ('dp', 'section'), route)]
where the time goes in v2:
time: 91 us; the launch traced here: 90.2 us
  blocking collectives  46.9 us (52%)
  starting transfers between devices  17 us (19%)
  waiting for transfers between devices  17 us (19%)
  Pallas kernels  7.87 us (9%)
    all_gather x1, blocking collectives, shards(): gathered = lax.all_gather(mine, 'tensor')  46.9 us
    ppermute x2, waiting for transfers between devices, exchange(): lax.ppermute(block, 'dp', [(i, i ^ bit) for i in range(lax.axis_size('dp'...  12.1 us
    ppermute x2, starting transfers between devices, along_section(): return lax.ppermute(block, 'section', route)  7.75 us
    ppermute x2, starting transfers between devices, exchange_along(): return lax.ppermute(block, ('dp', 'section'), route)  5.31 us
    ppermute x2, waiting for transfers between devices, exchange_along(): return lax.ppermute(block, ('dp', 'section'), route)  4.93 us
    ppermute x2, starting transfers between devices, exchange(): lax.ppermute(block, 'dp', [(i, i ^ bit) for i in range(lax.axis_size('dp'...  3.97 us
    pallas_call x1, Pallas kernels, partials(): pl.pallas_call(partials_kernel, out_shape=jax.ShapeDtypeStruct((tokens +...  3.65 us
    pallas_call x1, Pallas kernels, factors(): pl.pallas_call(factor_kernel, out_shape=(jax.ShapeDtypeStruct((width // 1...  2.67 us
  transfers between devices with their start and end apart: 6, of which 4 were waited for; matrix products, arithmetic and copies ran while one was open for 1% of the time, Pallas kernels for 4%

profile of v2, /device:TPU:24, one launch (start us, length us, event | category | flops | bytes accessed | tf_op | source)
XLA Modules:
  0.0 90.2 jit_solution(11010650788231656966)
XLA Ops:
  0.6 4.3 %collective-permute-start = (bf16[128,4096]{1,0:T(8,128)(2,1)}, bf16[128,4096]{1,0:T(8,128)(2,1)S(1)}, u32[]{:S(2)}, u32[]{:S(2)}) collective-permute-start(bf16[128,4096]{1,0:T(8,128)(2,1)} %bitcast.10), channel_id=1, source_target_pairs={{4,0},{8,4},{12,8},{16,12},{20,16},{24,20},{28,24},{32,28},{36,32}... | collective-permute-start | bytes 3145736 | tf_op jit(solution)/shard_map/ppermute | solution.py:296
  4.9 0.0 copy-start
  4.9 3.6 %partials.1 = bf16[200,128]{1,0:T(8,128)(2,1)} custom-call(bf16[128,4096]{1,0:T(8,128)(2,1)} %bitcast.8, bf16[128,4096]{1,0:T(8,128)(2,1)} %bitcast.11, bf16[1,4096]{1,0:T(2,128)(2,1)} %gain_ref.1, bf16[32,4096]{1,0:T(8,128)(2,1)} %bitcast.15), custom_call_target="tpu_custom_call" | custom-call | tf_op jit(solution)/shard_map/partials/pallas_call | solution.py:227
  8.6 46.9 %all-gather = bf16[800,128]{1,0:T(8,128)(2,1)S(1)} all-gather(bf16[200,128]{1,0:T(8,128)(2,1)} %partials.1), channel_id=2, replica_groups=mesh['dp'=8,'section'=32,'tensor'=4] {'tensor'}, dimensions={0}, use_global_device_ids=true | all-gather | bytes 256000 | tf_op jit(solution)/shard_map/all_gather | solution.py:320
  55.5 0.0 collective-permute-done.next_hbm
  55.5 0.0 copy-done
  55.5 0.0 copy-start.1
  55.5 0.0 copy-start.2
  55.5 2.7 %factors.1 = (f32[32,128]{1,0:T(8,128)S(1)}, bf16[32,128]{1,0:T(8,128)(2,1)}, bf16[32,128]{1,0:T(8,128)(2,1)S(1)}) custom-call(bf16[4,200,128]{2,1,0:T(8,128)(2,1)S(1)} %bitcast.13, bf16[128,4096]{1,0:T(8,128)(2,1)S(1)} %bitcast.9, bf16[128,4096]{1,0:T(8,128)(2,1)S(1)} %collective-permute-done.next_hbm), custom_call_target="tpu_custom_call" | custom-call | tf_op jit(solution)/shard_map/factors/pallas_call | solution.py:248
  58.2 0.0 copy-done.1
  58.2 0.0 copy-done.2
  58.2 0.3 coefficients.1
  58.5 3.5 %collective-permute-start.1 = (bf16[32,4224]{1,0:T(8,128)(2,1)S(1)}, bf16[32,4224]{1,0:T(8,128)(2,1)S(1)}, u32[]{:S(2)}, u32[]{:S(2)}) collective-permute-start(bf16[32,4224]{1,0:T(8,128)(2,1)S(1)} %coefficients.1), channel_id=1, source_target_pairs={{4,0},{8,4},{12,8},{16,12},{20,16},{24,20},{28,24},{32,28},{36,32}... | collective-permute-start | bytes 811016 | tf_op jit(solution)/shard_map/ppermute | solution.py:296
  62.0 2.1 %collective-permute-start.2 = (f32[32,128]{1,0:T(8,128)S(1)}, f32[32,128]{1,0:T(8,128)S(1)}, u32[]{:S(2)}, u32[]{:S(2)}) collective-permute-start(f32[32,128]{1,0:T(8,128)S(1)} %get-tuple-element.5), channel_id=1, source_target_pairs={{0,512},{128,640},{256,768},{384,896},{512,0},{640,128},{768,256},... | collective-permute-start | bytes 49160 | tf_op jit(solution)/shard_map/ppermute | solution.py:300
  64.1 7.5 %collective-permute-done.2 = f32[32,128]{1,0:T(8,128)S(1)} collective-permute-done((f32[32,128]{1,0:T(8,128)S(1)}, f32[32,128]{1,0:T(8,128)S(1)}, u32[]{:S(2)}, u32[]{:S(2)}) %collective-permute-start.2) | collective-permute-done | bytes 16416 | tf_op jit(solution)/shard_map/ppermute | solution.py:300
  71.5 1.9 %collective-permute-start.3 = (f32[32,128]{1,0:T(8,128)S(1)}, f32[32,128]{1,0:T(8,128)S(1)}, u32[]{:S(2)}, u32[]{:S(2)}) collective-permute-start(f32[32,128]{1,0:T(8,128)S(1)} %add.9), channel_id=1, source_target_pairs={{0,256},{128,384},{256,0},{384,128},{512,768},{640,896},{768,512},... | collective-permute-start | bytes 49160 | tf_op jit(solution)/shard_map/ppermute | solution.py:300
  73.5 4.6 %collective-permute-done.3 = f32[32,128]{1,0:T(8,128)S(1)} collective-permute-done((f32[32,128]{1,0:T(8,128)S(1)}, f32[32,128]{1,0:T(8,128)S(1)}, u32[]{:S(2)}, u32[]{:S(2)}) %collective-permute-start.3) | collective-permute-done | bytes 16416 | tf_op jit(solution)/shard_map/ppermute | solution.py:300
  78.1 1.9 %collective-permute-start.5 = (f32[32,128]{1,0:T(8,128)S(1)}, f32[32,128]{1,0:T(8,128)S(1)}, u32[]{:S(2)}, u32[]{:S(2)}) collective-permute-start(f32[32,128]{1,0:T(8,128)S(1)} %add.10), channel_id=1, source_target_pairs={{0,132},{4,136},{8,140},{12,144},{16,148},{20,152},{24,156},{28,16... | collective-permute-start | bytes 49160 | tf_op jit(solution)/shard_map/ppermute | solution.py:310
  80.0 3.4 %collective-permute-start.4 = (f32[32,128]{1,0:T(8,128)S(1)}, f32[32,128]{1,0:T(8,128)S(1)}, u32[]{:S(2)}, u32[]{:S(2)}) collective-permute-start(f32[32,128]{1,0:T(8,128)S(1)} %add.10), channel_id=1, source_target_pairs={{0,4},{4,8},{8,12},{12,16},{16,20},{20,24},{24,28},{28,32},{32,36}... | collective-permute-start | bytes 49160 | tf_op jit(solution)/shard_map/ppermute | solution.py:310
  83.4 2.7 %collective-permute-done.5 = f32[32,128]{1,0:T(8,128)S(1)} collective-permute-done((f32[32,128]{1,0:T(8,128)S(1)}, f32[32,128]{1,0:T(8,128)S(1)}, u32[]{:S(2)}, u32[]{:S(2)}) %collective-permute-start.5) | collective-permute-done | bytes 16416 | tf_op jit(solution)/shard_map/ppermute | solution.py:310
  86.1 2.2 %collective-permute-done.4 = f32[32,128]{1,0:T(8,128)S(1)} collective-permute-done((f32[32,128]{1,0:T(8,128)S(1)}, f32[32,128]{1,0:T(8,128)S(1)}, u32[]{:S(2)}, u32[]{:S(2)}) %collective-permute-start.4) | collective-permute-done | bytes 16416 | tf_op jit(solution)/shard_map/ppermute | solution.py:310
  88.3 0.6 add.11
  88.9 0.0 collective-permute-done.1.both_ref
  88.9 1.2 %rebuild.1 = bf16[128,4096]{1,0:T(8,128)(2,1)} custom-call(bf16[32,4224]{1,0:T(8,128)(2,1)S(1)} %collective-permute-done.1.both_ref), custom_call_target="tpu_custom_call" | custom-call | tf_op jit(solution)/shard_map/rebuild/pallas_call | solution.py:279
  (2 shorter events, 0.0 us)
Async XLA Ops:
  0.6 54.9 %collective-permute-start = (bf16[128,4096]{1,0:T(8,128)(2,1)}, bf16[128,4096]{1,0:T(8,128)(2,1)S(1)}, u32[]{:S(2)}, u32[]{:S(2)}) collective-permute-start(bf16[128,4096]{1,0:T(8,128)(2,1)} %bitcast.10), channel_id=1, source_target_pairs={{4,0},{8,4},{12,8},{16,12},{20,16},{24,20},{28,24},{32,28},{36,32}... | collective-permute-start | bytes 3145736 | tf_op jit(solution)/shard_map/ppermute | solution.py:296
  4.9 50.6 %copy-start = (bf16[1,128,4096]{2,1,0:T(8,128)(2,1)S(1)}, bf16[1,128,4096]{2,1,0:T(8,128)(2,1)}, u32[]{:S(2)}) copy-start(bf16[1,128,4096]{2,1,0:T(8,128)(2,1)} %param.4) | copy-start | bytes 3145732
  55.5 2.7 %copy-start.1 = (bf16[1,128,4096]{2,1,0:T(8,128)(2,1)S(1)}, bf16[1,128,4096]{2,1,0:T(8,128)(2,1)}, u32[]{:S(2)}) copy-start(bf16[1,128,4096]{2,1,0:T(8,128)(2,1)} %param.7) | copy-start | bytes 3145732
  55.5 2.7 %copy-start.2 = (bf16[1,4096]{1,0:T(2,128)(2,1)S(1)}, bf16[1,4096]{1,0:T(2,128)(2,1)}, u32[]{:S(2)}) copy-start(bf16[1,4096]{1,0:T(2,128)(2,1)} %gain_ref.1) | copy-start | bytes 24580
  58.5 30.4 %collective-permute-start.1 = (bf16[32,4224]{1,0:T(8,128)(2,1)S(1)}, bf16[32,4224]{1,0:T(8,128)(2,1)S(1)}, u32[]{:S(2)}, u32[]{:S(2)}) collective-permute-start(bf16[32,4224]{1,0:T(8,128)(2,1)S(1)} %coefficients.1), channel_id=1, source_target_pairs={{4,0},{8,4},{12,8},{16,12},{20,16},{24,20},{28,24},{32,28},{36,32}... | collective-permute-start | bytes 811016 | tf_op jit(solution)/shard_map/ppermute | solution.py:296
  62.0 9.5 %collective-permute-start.2 = (f32[32,128]{1,0:T(8,128)S(1)}, f32[32,128]{1,0:T(8,128)S(1)}, u32[]{:S(2)}, u32[]{:S(2)}) collective-permute-start(f32[32,128]{1,0:T(8,128)S(1)} %get-tuple-element.5), channel_id=1, source_target_pairs={{0,512},{128,640},{256,768},{384,896},{512,0},{640,128},{768,256},... | collective-permute-start | bytes 49160 | tf_op jit(solution)/shard_map/ppermute | solution.py:300
  71.5 6.5 %collective-permute-start.3 = (f32[32,128]{1,0:T(8,128)S(1)}, f32[32,128]{1,0:T(8,128)S(1)}, u32[]{:S(2)}, u32[]{:S(2)}) collective-permute-start(f32[32,128]{1,0:T(8,128)S(1)} %add.9), channel_id=1, source_target_pairs={{0,256},{128,384},{256,0},{384,128},{512,768},{640,896},{768,512},... | collective-permute-start | bytes 49160 | tf_op jit(solution)/shard_map/ppermute | solution.py:300
  78.1 8.1 %collective-permute-start.5 = (f32[32,128]{1,0:T(8,128)S(1)}, f32[32,128]{1,0:T(8,128)S(1)}, u32[]{:S(2)}, u32[]{:S(2)}) collective-permute-start(f32[32,128]{1,0:T(8,128)S(1)} %add.10), channel_id=1, source_target_pairs={{0,132},{4,136},{8,140},{12,144},{16,148},{20,152},{24,156},{28,16... | collective-permute-start | bytes 49160 | tf_op jit(solution)/shard_map/ppermute | solution.py:310
  80.0 8.3 %collective-permute-start.4 = (f32[32,128]{1,0:T(8,128)S(1)}, f32[32,128]{1,0:T(8,128)S(1)}, u32[]{:S(2)}, u32[]{:S(2)}) collective-permute-start(f32[32,128]{1,0:T(8,128)S(1)} %add.10), channel_id=1, source_target_pairs={{0,4},{4,8},{8,12},{12,16},{16,20},{20,24},{24,28},{28,32},{32,36}... | collective-permute-start | bytes 49160 | tf_op jit(solution)/shard_map/ppermute | solution.py:310

commit v3 on v2

--- a/solution.py
+++ b/solution.py
@@ -155,7 +155,7 @@
 
 
 def factor_kernel(
-    gathered_ref, rows_hbm, next_hbm, local_ref, forward_ref, backward_ref, rows_ref, next_ref, sems
+    gathered_ref, rows_hbm, next_hbm, spread_ref, backward_ref, local_ref, rows_ref, next_ref, sems
 ):
     copies = [
         pltpu.make_async_copy(rows_hbm, rows_ref, sems.at[0]),
@@ -177,7 +177,6 @@
         gram = unpacked(total[turn * half : (turn + 1) * half], diagonal)
         pairs.append(orthonormal(gram, total[at : at + rank]))
     forward, backward = (basis.astype(BF16) for basis in eliminate(pairs))
-    forward_ref[...] = forward
     backward_ref[...] = backward
     for copy in copies:
         copy.wait()
@@ -191,6 +190,9 @@
         for lane in range(0, chunk, 128):
             at = (start + lane) // 128
             local_ref[at : at + 1] = summed[:, lane : lane + 128]
+    local = local_ref[...].astype(BF16)
+    for i in range(spread_ref.shape[0]):
+        spread_ref[i] = local
 
 
 def coeff_kernel(basis_ref, grad_ref, gain_ref, out_ref):
@@ -240,17 +242,18 @@
     )(rows, grad, gain, sketch_rows)
 
 
-def factors(gathered, rows, next_grad, rank):
+def factors(gathered, rows, next_grad, rank, copies):
     tokens, width = rows.shape
     vmem = pl.BlockSpec(memory_space=pltpu.VMEM)
     anywhere = pl.BlockSpec(memory_space=pl.ANY)
     basis = jax.ShapeDtypeStruct((rank, tokens), BF16)
     return pl.pallas_call(
         factor_kernel,
-        out_shape=(jax.ShapeDtypeStruct((width // 128, 128), F32), basis, basis),
+        out_shape=(jax.ShapeDtypeStruct((copies, width // 128, 128), BF16), basis),
         in_specs=[vmem, anywhere, anywhere],
-        out_specs=(vmem, vmem, vmem),
+        out_specs=(vmem, vmem),
         scratch_shapes=[
+            pltpu.VMEM((width // 128, 128), F32),
             pltpu.VMEM((tokens, width), BF16),
             pltpu.VMEM((tokens, width), BF16),
             pltpu.SemaphoreType.DMA((2,)),
@@ -296,20 +299,6 @@
     return lax.ppermute(block, "section", route)
 
 
-def exchange(block, bit):
-    return lax.ppermute(block, "dp", [(i, i ^ bit) for i in range(lax.axis_size("dp"))])
-
-
-def exchange_along(block, bit):
-    sections, members = lax.axis_size("section"), lax.axis_size("dp")
-    route = [
-        (i * sections + s, (i ^ bit) * sections + s + 1)
-        for i in range(members)
-        for s in range(sections - 1)
-    ]
-    return lax.ppermute(block, ("dp", "section"), route)
-
-
 def shards(section_output, sketch_matrix, boundary_gain, grad_gained):
     rows = section_output[0]
     sketch_rows = sketch_matrix[0].T
@@ -318,16 +307,12 @@
     next_grad = along_section(grad, -1)
     mine = partials(rows, grad, boundary_gain, sketch_rows)
     gathered = lax.all_gather(mine, "tensor")
-    local, _, backward = factors(gathered, rows, next_grad, sketch_rows.shape[0])
-    far = exchange(local, 4)
+    local, backward = factors(gathered, rows, next_grad, sketch_rows.shape[0], lax.axis_size("dp"))
     both = coefficients(backward, grad, boundary_gain)
     both = along_section(both, -1)
-    summed = local + far
-    middle = exchange(summed, 2)
-    summed = summed + middle
-    own = exchange_along(summed, 0)
-    near = exchange_along(summed, 1)
-    gain_grad = own + near
+    locals_ = lax.all_to_all(local, "dp", 0, 0)
+    summed = jnp.sum(locals_.astype(F32), axis=0)
+    gain_grad = along_section(summed, 1)
     grad_output = rebuild(both, tokens)
     return grad_output[None], gain_grad.reshape(1, -1)
 

time: 91 us -> 81.4 us (0.89)
  waiting for transfers between devices: 17 us -> 11.5 us
  starting transfers between devices: 17 us -> 13 us
    ppermute x4 -> x0, waiting for transfers between devices: 17 us -> none  [the longest x2 12.1 us: exchange(): lax.ppermute(block, 'dp', [(i, i ^ bit) for i in range(lax.axis_size('dp'...]
    ppermute x4 -> x0, starting transfers between devices: 9.27 us -> none  [the longest x2 5.31 us: exchange_along(): return lax.ppermute(block, ('dp', 'section'), route)]
    all_to_all x0 -> x1, waiting for transfers between devices: none -> 7.5 us  [shards(): locals_ = lax.all_to_all(local, 'dp', 0, 0)]
    ppermute x2 -> x3, waiting for transfers between devices: 0.01 us -> 3.98 us  [along_section(): return lax.ppermute(block, 'section', route)]
    all_to_all x0 -> x1, starting transfers between devices: none -> 3.77 us  [shards(): locals_ = lax.all_to_all(local, 'dp', 0, 0)]
    ppermute x2 -> x3, starting transfers between devices: 7.75 us -> 9.27 us  [along_section(): return lax.ppermute(block, 'section', route)]
  transfers between devices with their start and end apart: 6 -> 4, of which waited for: 4 -> 2; matrix products, arithmetic and copies ran while one was open for 1% -> 0% of each run, Pallas kernels for 4% -> 6%
where the time goes in v3:
time: 81.4 us; the launch traced here: 81.1 us
  blocking collectives  46.9 us (58%)
  starting transfers between devices  13 us (16%)
  waiting for transfers between devices  11.5 us (14%)
  Pallas kernels  8.33 us (10%)
    all_gather x1, blocking collectives, shards(): gathered = lax.all_gather(mine, 'tensor')  46.9 us
    ppermute x3, starting transfers between devices, along_section(): return lax.ppermute(block, 'section', route)  9.27 us
    all_to_all x1, waiting for transfers between devices, shards(): locals_ = lax.all_to_all(local, 'dp', 0, 0)  7.5 us
    ppermute x3, waiting for transfers between devices, along_section(): return lax.ppermute(block, 'section', route)  3.98 us
    all_to_all x1, starting transfers between devices, shards(): locals_ = lax.all_to_all(local, 'dp', 0, 0)  3.77 us
    pallas_call x1, Pallas kernels, partials(): pl.pallas_call(partials_kernel, out_shape=jax.ShapeDtypeStruct((tokens +...  3.65 us
    pallas_call x1, Pallas kernels, factors(): pl.pallas_call(factor_kernel, out_shape=(jax.ShapeDtypeStruct((copies, wi...  3.13 us
  transfers between devices with their start and end apart: 4, of which 2 were waited for; matrix products, arithmetic and copies ran while one was open for 0% of the time, Pallas kernels for 6%

profile of v3, /device:TPU:24, one launch (start us, length us, event | category | flops | bytes accessed | tf_op | source)
XLA Modules:
  0.0 81.1 jit_solution(16594390369502208005)
XLA Ops:
  0.6 4.3 %collective-permute-start = (bf16[128,4096]{1,0:T(8,128)(2,1)}, bf16[128,4096]{1,0:T(8,128)(2,1)S(1)}, u32[]{:S(2)}, u32[]{:S(2)}) collective-permute-start(bf16[128,4096]{1,0:T(8,128)(2,1)} %bitcast.10), channel_id=1, source_target_pairs={{4,0},{8,4},{12,8},{16,12},{20,16},{24,20},{28,24},{32,28},{36,32}... | collective-permute-start | bytes 3145736 | tf_op jit(solution)/shard_map/ppermute | solution.py:299
  4.9 0.0 copy-start
  4.9 3.6 %partials.1 = bf16[200,128]{1,0:T(8,128)(2,1)} custom-call(bf16[128,4096]{1,0:T(8,128)(2,1)} %bitcast.8, bf16[128,4096]{1,0:T(8,128)(2,1)} %bitcast.11, bf16[1,4096]{1,0:T(2,128)(2,1)} %gain_ref.1, bf16[32,4096]{1,0:T(8,128)(2,1)} %bitcast.15), custom_call_target="tpu_custom_call" | custom-call | tf_op jit(solution)/shard_map/partials/pallas_call | solution.py:229
  8.6 46.9 %all-gather = bf16[800,128]{1,0:T(8,128)(2,1)S(1)} all-gather(bf16[200,128]{1,0:T(8,128)(2,1)} %partials.1), channel_id=2, replica_groups=mesh['dp'=8,'section'=32,'tensor'=4] {'tensor'}, dimensions={0}, use_global_device_ids=true | all-gather | bytes 256000 | tf_op jit(solution)/shard_map/all_gather | solution.py:309
  55.5 0.0 collective-permute-done.next_hbm
  55.5 0.0 copy-done
  55.5 0.0 copy-start.1
  55.5 3.1 %factors.1 = (bf16[8,32,128]{2,1,0:T(8,128)(2,1)}, bf16[32,128]{1,0:T(8,128)(2,1)S(1)}) custom-call(bf16[4,200,128]{2,1,0:T(8,128)(2,1)S(1)} %bitcast.13, bf16[128,4096]{1,0:T(8,128)(2,1)S(1)} %bitcast.9, bf16[128,4096]{1,0:T(8,128)(2,1)S(1)} %collective-permute-done.next_hbm), custom_call_target="tpu_custom_call" | custom-call | tf_op jit(solution)/shard_map/factors/pallas_call | solution.py:250
  58.6 0.0 copy-start.2
  58.7 3.8 %all-to-all-start = ((bf16[8,32,128]{2,1,0:T(8,128)(2,1)}), bf16[8,32,128]{2,1,0:T(8,128)(2,1)S(1)}, u32[]{:S(2)}, u32[]{:S(2)}) async-start(bf16[8,32,128]{2,1,0:T(8,128)(2,1)} %get-tuple-element.5), calls=%async_computation | async-start | bytes 131072 | tf_op jit(solution)/shard_map/all_to_all | solution.py:313
  62.4 0.0 copy-done.1
  62.4 0.0 copy-done.2
  62.4 0.3 coefficients.1
  62.7 3.1 %collective-permute-start.1 = (bf16[32,4224]{1,0:T(8,128)(2,1)S(1)}, bf16[32,4224]{1,0:T(8,128)(2,1)S(1)}, u32[]{:S(2)}, u32[]{:S(2)}) collective-permute-start(bf16[32,4224]{1,0:T(8,128)(2,1)S(1)} %coefficients.1), channel_id=1, source_target_pairs={{4,0},{8,4},{12,8},{16,12},{20,16},{24,20},{28,24},{32,28},{36,32}... | collective-permute-start | bytes 811016 | tf_op jit(solution)/shard_map/ppermute | solution.py:299
  65.8 7.5 %all-to-all-done = bf16[8,32,128]{2,1,0:T(8,128)(2,1)S(1)} async-done(((bf16[8,32,128]{2,1,0:T(8,128)(2,1)}), bf16[8,32,128]{2,1,0:T(8,128)(2,1)S(1)}, u32[]{:S(2)}, u32[]{:S(2)}) %all-to-all-start) | async-done | bytes 65568 | tf_op jit(solution)/shard_map/all_to_all | solution.py:313
  73.3 1.9 %collective-permute-start.2 = (f32[32,128]{1,0:T(8,128)S(1)}, f32[32,128]{1,0:T(8,128)S(1)}, u32[]{:S(2)}, u32[]{:S(2)}) collective-permute-start(f32[32,128]{1,0:T(8,128)S(1)} %convert_reduce_fusion), channel_id=1, source_target_pairs={{0,4},{4,8},{8,12},{12,16},{16,20},{20,24},{24,28},{28,32},{32,36}... | collective-permute-start | bytes 49160 | tf_op jit(solution)/shard_map/ppermute | solution.py:299
  75.3 0.0 collective-permute-done.1.both_ref
  75.3 1.2 %rebuild.1 = bf16[128,4096]{1,0:T(8,128)(2,1)} custom-call(bf16[32,4224]{1,0:T(8,128)(2,1)S(1)} %collective-permute-done.1.both_ref), custom_call_target="tpu_custom_call" | custom-call | tf_op jit(solution)/shard_map/rebuild/pallas_call | solution.py:282
  76.5 4.0 %collective-permute-done.2 = f32[32,128]{1,0:T(8,128)S(1)} collective-permute-done((f32[32,128]{1,0:T(8,128)S(1)}, f32[32,128]{1,0:T(8,128)S(1)}, u32[]{:S(2)}, u32[]{:S(2)}) %collective-permute-start.2) | collective-permute-done | bytes 16416 | tf_op jit(solution)/shard_map/ppermute | solution.py:299
  80.5 0.6 copy.7
  (1 shorter events, 0.0 us)
Async XLA Ops:
  0.6 54.9 %collective-permute-start = (bf16[128,4096]{1,0:T(8,128)(2,1)}, bf16[128,4096]{1,0:T(8,128)(2,1)S(1)}, u32[]{:S(2)}, u32[]{:S(2)}) collective-permute-start(bf16[128,4096]{1,0:T(8,128)(2,1)} %bitcast.10), channel_id=1, source_target_pairs={{4,0},{8,4},{12,8},{16,12},{20,16},{24,20},{28,24},{32,28},{36,32}... | collective-permute-start | bytes 3145736 | tf_op jit(solution)/shard_map/ppermute | solution.py:299
  4.9 50.6 %copy-start = (bf16[1,128,4096]{2,1,0:T(8,128)(2,1)S(1)}, bf16[1,128,4096]{2,1,0:T(8,128)(2,1)}, u32[]{:S(2)}) copy-start(bf16[1,128,4096]{2,1,0:T(8,128)(2,1)} %param.4) | copy-start | bytes 3145732
  55.5 6.9 %copy-start.1 = (bf16[1,128,4096]{2,1,0:T(8,128)(2,1)S(1)}, bf16[1,128,4096]{2,1,0:T(8,128)(2,1)}, u32[]{:S(2)}) copy-start(bf16[1,128,4096]{2,1,0:T(8,128)(2,1)} %param.7) | copy-start | bytes 3145732
  58.6 3.8 %copy-start.2 = (bf16[1,4096]{1,0:T(2,128)(2,1)S(1)}, bf16[1,4096]{1,0:T(2,128)(2,1)}, u32[]{:S(2)}) copy-start(bf16[1,4096]{1,0:T(2,128)(2,1)} %gain_ref.1) | copy-start | bytes 24580
  58.7 14.7 %all-to-all-start = ((bf16[8,32,128]{2,1,0:T(8,128)(2,1)}), bf16[8,32,128]{2,1,0:T(8,128)(2,1)S(1)}, u32[]{:S(2)}, u32[]{:S(2)}) async-start(bf16[8,32,128]{2,1,0:T(8,128)(2,1)} %get-tuple-element.5), calls=%async_computation | async-start | bytes 131072 | tf_op jit(solution)/shard_map/all_to_all | solution.py:313
  62.7 12.5 %collective-permute-start.1 = (bf16[32,4224]{1,0:T(8,128)(2,1)S(1)}, bf16[32,4224]{1,0:T(8,128)(2,1)S(1)}, u32[]{:S(2)}, u32[]{:S(2)}) collective-permute-start(bf16[32,4224]{1,0:T(8,128)(2,1)S(1)} %coefficients.1), channel_id=1, source_target_pairs={{4,0},{8,4},{12,8},{16,12},{20,16},{24,20},{28,24},{32,28},{36,32}... | collective-permute-start | bytes 811016 | tf_op jit(solution)/shard_map/ppermute | solution.py:299
  73.3 7.2 %collective-permute-start.2 = (f32[32,128]{1,0:T(8,128)S(1)}, f32[32,128]{1,0:T(8,128)S(1)}, u32[]{:S(2)}, u32[]{:S(2)}) collective-permute-start(f32[32,128]{1,0:T(8,128)S(1)} %convert_reduce_fusion), channel_id=1, source_target_pairs={{0,4},{4,8},{8,12},{12,16},{16,20},{20,24},{24,28},{28,32},{32,36}... | collective-permute-start | bytes 49160 | tf_op jit(solution)/shard_map/ppermute | solution.py:299

commit v4 on v3

--- a/solution.py
+++ b/solution.py
@@ -48,7 +48,17 @@
 
 
 def partials_kernel(
-    rows_hbm, grad_hbm, gain_hbm, sketch_hbm, out_ref, rows_ref, grad_ref, gain_ref, sketch_ref, sems
+    rows_hbm,
+    grad_hbm,
+    gain_hbm,
+    sketch_hbm,
+    copies_ref,
+    out_ref,
+    rows_ref,
+    grad_ref,
+    gain_ref,
+    sketch_ref,
+    sems,
 ):
     tokens, width = rows_ref.shape
     rank = sketch_ref.shape[0]
@@ -100,6 +110,8 @@
     rest = jnp.zeros((out_ref.shape[0] - 2 * half - 2 * rank - 4, tokens), F32)
     tail = jnp.concatenate(diagonals + [rest], axis=0)
     out_ref[2 * half + 2 * rank :] = tail.astype(BF16)
+    for copy in range(copies_ref.shape[0]):
+        copies_ref[copy] = out_ref[...]
 
 
 def orthonormal(gram, first):
@@ -222,16 +234,17 @@
         copy.wait()
 
 
-def partials(rows, grad, gain, sketch_rows):
+def partials(rows, grad, gain, sketch_rows, copies):
     tokens, width = rows.shape
     rank = sketch_rows.shape[0]
     anywhere = pl.BlockSpec(memory_space=pl.ANY)
     return pl.pallas_call(
         partials_kernel,
-        out_shape=jax.ShapeDtypeStruct((tokens + 2 * rank + 8, tokens), BF16),
+        out_shape=jax.ShapeDtypeStruct((copies, tokens + 2 * rank + 8, tokens), BF16),
         in_specs=[anywhere] * 4,
         out_specs=pl.BlockSpec(memory_space=pltpu.VMEM),
         scratch_shapes=[
+            pltpu.VMEM((tokens + 2 * rank + 8, tokens), BF16),
             pltpu.VMEM((tokens, width), BF16),
             pltpu.VMEM((tokens, width), BF16),
             pltpu.VMEM((1, width), BF16),
@@ -305,9 +318,12 @@
     grad = grad_gained[0]
     tokens = rows.shape[0]
     next_grad = along_section(grad, -1)
-    mine = partials(rows, grad, boundary_gain, sketch_rows)
-    gathered = lax.all_gather(mine, "tensor")
-    local, backward = factors(gathered, rows, next_grad, sketch_rows.shape[0], lax.axis_size("dp"))
+    members = lax.axis_size("tensor")
+    mine = partials(rows, grad, boundary_gain, sketch_rows, members)
+    gathered = lax.all_to_all(mine, "tensor", 0, 0)
+    local, backward = factors(
+        gathered, rows, next_grad, sketch_rows.shape[0], lax.axis_size("dp")
+    )
     both = coefficients(backward, grad, boundary_gain)
     both = along_section(both, -1)
     locals_ = lax.all_to_all(local, "dp", 0, 0)

time: 81.4 us -> 96.7 us (1.19)
  blocking collectives: 46.9 us -> 0 us
  starting transfers between devices: 13 us -> 47.1 us
  waiting for transfers between devices: 11.5 us -> 39.4 us
    all_gather x1 -> x0, blocking collectives: 46.9 us -> none  [shards(): gathered = lax.all_gather(mine, 'tensor')]
    all_to_all x0 -> x1, starting transfers between devices: none -> 28.3 us  [shards(): gathered = lax.all_to_all(mine, 'tensor', 0, 0)]
    all_to_all x0 -> x1, waiting for transfers between devices: none -> 14.5 us  [shards(): gathered = lax.all_to_all(mine, 'tensor', 0, 0)]
    ppermute x3, waiting for transfers between devices: 3.98 us -> 16.3 us  [along_section(): return lax.ppermute(block, 'section', route)]
    all_to_all x1, starting transfers between devices: 3.77 us -> 11 us  [shards(): locals_ = lax.all_to_all(local, 'dp', 0, 0)]
    ppermute x3, starting transfers between devices: 9.27 us -> 7.84 us  [along_section(): return lax.ppermute(block, 'section', route)]
    all_to_all x1, waiting for transfers between devices: 7.5 us -> 8.65 us  [shards(): locals_ = lax.all_to_all(local, 'dp', 0, 0)]
  transfers between devices with their start and end apart: 4 -> 5, of which waited for: 2 -> 4; matrix products, arithmetic and copies ran while one was open for 0% -> 0% of each run, Pallas kernels for 6% -> 2%
where the time goes in v4:
time: 96.7 us; the launch traced here: 96.3 us
  starting transfers between devices  47.1 us (49%)
  waiting for transfers between devices  39.4 us (41%)
  Pallas kernels  8.46 us (9%)
    all_to_all x1, starting transfers between devices, shards(): gathered = lax.all_to_all(mine, 'tensor', 0, 0)  28.3 us
    ppermute x3, waiting for transfers between devices, along_section(): return lax.ppermute(block, 'section', route)  16.3 us
    all_to_all x1, waiting for transfers between devices, shards(): gathered = lax.all_to_all(mine, 'tensor', 0, 0)  14.5 us
    all_to_all x1, starting transfers between devices, shards(): locals_ = lax.all_to_all(local, 'dp', 0, 0)  11 us
    all_to_all x1, waiting for transfers between devices, shards(): locals_ = lax.all_to_all(local, 'dp', 0, 0)  8.65 us
    ppermute x3, starting transfers between devices, along_section(): return lax.ppermute(block, 'section', route)  7.84 us
    pallas_call x1, Pallas kernels, partials(): pl.pallas_call(partials_kernel, out_shape=jax.ShapeDtypeStruct((copies, t...  3.78 us
    pallas_call x1, Pallas kernels, factors(): pl.pallas_call(factor_kernel, out_shape=(jax.ShapeDtypeStruct((copies, wi...  3.13 us
  transfers between devices with their start and end apart: 5, of which 4 were waited for; matrix products, arithmetic and copies ran while one was open for 0% of the time, Pallas kernels for 2%

profile of v4, /device:TPU:24, one launch (start us, length us, event | category | flops | bytes accessed | tf_op | source)
XLA Modules:
  0.0 96.3 jit_solution(7859441408546281975)
XLA Ops:
  0.6 0.0 copy-start.1
  0.6 0.0 copy-start
  0.6 3.8 %partials.1 = bf16[4,200,128]{2,1,0:T(8,128)(2,1)} custom-call(bf16[128,4096]{1,0:T(8,128)(2,1)} %bitcast.7, bf16[128,4096]{1,0:T(8,128)(2,1)} %bitcast.9, bf16[1,4096]{1,0:T(2,128)(2,1)} %gain_ref.1, bf16[32,4096]{1,0:T(8,128)(2,1)} %bitcast.13), custom_call_target="tpu_custom_call" | custom-call | tf_op jit(solution)/shard_map/partials/pallas_call | solution.py:241
  4.4 28.3 %all-to-all-start = ((bf16[4,200,128]{2,1,0:T(8,128)(2,1)}), bf16[4,200,128]{2,1,0:T(8,128)(2,1)S(1)}, u32[]{:S(2)}, u32[]{:S(2)}) async-start(bf16[4,200,128]{2,1,0:T(8,128)(2,1)} %partials.1), calls=%async_computation | async-start | bytes 409600 | tf_op jit(solution)/shard_map/all_to_all | solution.py:323
  32.8 0.0 copy-done.1
  32.8 4.0 %collective-permute-start = (bf16[128,4096]{1,0:T(8,128)(2,1)S(1)}, bf16[128,4096]{1,0:T(8,128)(2,1)S(1)}, u32[]{:S(2)}, u32[]{:S(2)}) collective-permute-start(bf16[128,4096]{1,0:T(8,128)(2,1)S(1)} %bitcast.10), channel_id=1, source_target_pairs={{4,0},{8,4},{12,8},{16,12},{20,16},{24,20},{28,24},{32,28},{36,32}... | collective-permute-start | bytes 3145736 | tf_op jit(solution)/shard_map/ppermute | solution.py:312
  36.8 12.3 %collective-permute-done.next_hbm = bf16[128,4096]{1,0:T(8,128)(2,1)S(1)} collective-permute-done((bf16[128,4096]{1,0:T(8,128)(2,1)S(1)}, bf16[128,4096]{1,0:T(8,128)(2,1)S(1)}, u32[]{:S(2)}, u32[]{:S(2)}) %collective-permute-start) | collective-permute-done | bytes 1048608 | tf_op jit(solution)/shard_map/ppermute | solution.py:312
  49.1 14.5 %all-to-all-done.gathered_ref = bf16[4,200,128]{2,1,0:T(8,128)(2,1)S(1)} async-done(((bf16[4,200,128]{2,1,0:T(8,128)(2,1)}), bf16[4,200,128]{2,1,0:T(8,128)(2,1)S(1)}, u32[]{:S(2)}, u32[]{:S(2)}) %all-to-all-start) | async-done | bytes 204832 | tf_op jit(solution)/shard_map/all_to_all | solution.py:323
  63.5 0.0 copy-done
  63.5 3.1 %factors.1 = (bf16[8,32,128]{2,1,0:T(8,128)(2,1)}, bf16[32,128]{1,0:T(8,128)(2,1)S(1)}) custom-call(bf16[4,200,128]{2,1,0:T(8,128)(2,1)S(1)} %all-to-all-done.gathered_ref, bf16[128,4096]{1,0:T(8,128)(2,1)S(1)} %bitcast.8, bf16[128,4096]{1,0:T(8,128)(2,1)S(1)} %collective-permute-done.next_hbm), custom_call_target="tpu_custom_call" | custom-call | tf_op jit(solution)/shard_map/factors/pallas_call | solution.py:263
  66.7 0.0 copy-start.2
  66.7 11.0 %all-to-all-start.1 = ((bf16[8,32,128]{2,1,0:T(8,128)(2,1)}), bf16[8,32,128]{2,1,0:T(8,128)(2,1)S(1)}, u32[]{:S(2)}, u32[]{:S(2)}) async-start(bf16[8,32,128]{2,1,0:T(8,128)(2,1)} %get-tuple-element.5), calls=%async_computation.1 | async-start | bytes 131072 | tf_op jit(solution)/shard_map/all_to_all | solution.py:329
  77.6 0.0 copy-done.2
  77.7 0.3 coefficients.1
  78.0 1.9 %collective-permute-start.1 = (bf16[32,4224]{1,0:T(8,128)(2,1)S(1)}, bf16[32,4224]{1,0:T(8,128)(2,1)S(1)}, u32[]{:S(2)}, u32[]{:S(2)}) collective-permute-start(bf16[32,4224]{1,0:T(8,128)(2,1)S(1)} %coefficients.1), channel_id=1, source_target_pairs={{4,0},{8,4},{12,8},{16,12},{20,16},{24,20},{28,24},{32,28},{36,32}... | collective-permute-start | bytes 811016 | tf_op jit(solution)/shard_map/ppermute | solution.py:312
  79.9 8.7 %all-to-all-done.1 = bf16[8,32,128]{2,1,0:T(8,128)(2,1)S(1)} async-done(((bf16[8,32,128]{2,1,0:T(8,128)(2,1)}), bf16[8,32,128]{2,1,0:T(8,128)(2,1)S(1)}, u32[]{:S(2)}, u32[]{:S(2)}) %all-to-all-start.1) | async-done | bytes 65568 | tf_op jit(solution)/shard_map/all_to_all | solution.py:329
  88.6 1.9 %collective-permute-start.2 = (f32[32,128]{1,0:T(8,128)S(1)}, f32[32,128]{1,0:T(8,128)S(1)}, u32[]{:S(2)}, u32[]{:S(2)}) collective-permute-start(f32[32,128]{1,0:T(8,128)S(1)} %convert_reduce_fusion), channel_id=1, source_target_pairs={{0,4},{4,8},{8,12},{12,16},{16,20},{20,24},{24,28},{28,32},{32,36}... | collective-permute-start | bytes 49160 | tf_op jit(solution)/shard_map/ppermute | solution.py:312
  90.5 0.0 collective-permute-done.1.both_ref
  90.5 1.2 %rebuild.1 = bf16[128,4096]{1,0:T(8,128)(2,1)} custom-call(bf16[32,4224]{1,0:T(8,128)(2,1)S(1)} %collective-permute-done.1.both_ref), custom_call_target="tpu_custom_call" | custom-call | tf_op jit(solution)/shard_map/rebuild/pallas_call | solution.py:295
  91.8 4.0 %collective-permute-done.2 = f32[32,128]{1,0:T(8,128)S(1)} collective-permute-done((f32[32,128]{1,0:T(8,128)S(1)}, f32[32,128]{1,0:T(8,128)S(1)}, u32[]{:S(2)}, u32[]{:S(2)}) %collective-permute-start.2) | collective-permute-done | bytes 16416 | tf_op jit(solution)/shard_map/ppermute | solution.py:312
  95.7 0.6 copy.7
  (1 shorter events, 0.0 us)
Async XLA Ops:
  0.6 32.2 %copy-start.1 = (bf16[1,128,4096]{2,1,0:T(8,128)(2,1)S(1)}, bf16[1,128,4096]{2,1,0:T(8,128)(2,1)}, u32[]{:S(2)}) copy-start(bf16[1,128,4096]{2,1,0:T(8,128)(2,1)} %param.7) | copy-start | bytes 3145732
  0.6 62.9 %copy-start = (bf16[1,128,4096]{2,1,0:T(8,128)(2,1)S(1)}, bf16[1,128,4096]{2,1,0:T(8,128)(2,1)}, u32[]{:S(2)}) copy-start(bf16[1,128,4096]{2,1,0:T(8,128)(2,1)} %param.4) | copy-start | bytes 3145732
  4.4 59.1 %all-to-all-start = ((bf16[4,200,128]{2,1,0:T(8,128)(2,1)}), bf16[4,200,128]{2,1,0:T(8,128)(2,1)S(1)}, u32[]{:S(2)}, u32[]{:S(2)}) async-start(bf16[4,200,128]{2,1,0:T(8,128)(2,1)} %partials.1), calls=%async_computation | async-start | bytes 409600 | tf_op jit(solution)/shard_map/all_to_all | solution.py:323
  32.8 16.3 %collective-permute-start = (bf16[128,4096]{1,0:T(8,128)(2,1)S(1)}, bf16[128,4096]{1,0:T(8,128)(2,1)S(1)}, u32[]{:S(2)}, u32[]{:S(2)}) collective-permute-start(bf16[128,4096]{1,0:T(8,128)(2,1)S(1)} %bitcast.10), channel_id=1, source_target_pairs={{4,0},{8,4},{12,8},{16,12},{20,16},{24,20},{28,24},{32,28},{36,32}... | collective-permute-start | bytes 3145736 | tf_op jit(solution)/shard_map/ppermute | solution.py:312
  66.7 11.0 %copy-start.2 = (bf16[1,4096]{1,0:T(2,128)(2,1)S(1)}, bf16[1,4096]{1,0:T(2,128)(2,1)}, u32[]{:S(2)}) copy-start(bf16[1,4096]{1,0:T(2,128)(2,1)} %gain_ref.1) | copy-start | bytes 24580
  66.7 21.9 %all-to-all-start.1 = ((bf16[8,32,128]{2,1,0:T(8,128)(2,1)}), bf16[8,32,128]{2,1,0:T(8,128)(2,1)S(1)}, u32[]{:S(2)}, u32[]{:S(2)}) async-start(bf16[8,32,128]{2,1,0:T(8,128)(2,1)} %get-tuple-element.5), calls=%async_computation.1 | async-start | bytes 131072 | tf_op jit(solution)/shard_map/all_to_all | solution.py:329
  78.0 12.5 %collective-permute-start.1 = (bf16[32,4224]{1,0:T(8,128)(2,1)S(1)}, bf16[32,4224]{1,0:T(8,128)(2,1)S(1)}, u32[]{:S(2)}, u32[]{:S(2)}) collective-permute-start(bf16[32,4224]{1,0:T(8,128)(2,1)S(1)} %coefficients.1), channel_id=1, source_target_pairs={{4,0},{8,4},{12,8},{16,12},{20,16},{24,20},{28,24},{32,28},{36,32}... | collective-permute-start | bytes 811016 | tf_op jit(solution)/shard_map/ppermute | solution.py:312
  88.6 7.2 %collective-permute-start.2 = (f32[32,128]{1,0:T(8,128)S(1)}, f32[32,128]{1,0:T(8,128)S(1)}, u32[]{:S(2)}, u32[]{:S(2)}) collective-permute-start(f32[32,128]{1,0:T(8,128)S(1)} %convert_reduce_fusion), channel_id=1, source_target_pairs={{0,4},{4,8},{8,12},{12,16},{16,20},{20,24},{24,28},{28,32},{32,36}... | collective-permute-start | bytes 49160 | tf_op jit(solution)/shard_map/ppermute | solution.py:312

commit v5 on v3

--- a/solution.py
+++ b/solution.py
@@ -154,17 +154,8 @@
     return [jnp.concatenate(finished, axis=0) for finished in done]
 
 
-def factor_kernel(
-    gathered_ref, rows_hbm, next_hbm, spread_ref, backward_ref, local_ref, rows_ref, next_ref, sems
-):
-    copies = [
-        pltpu.make_async_copy(rows_hbm, rows_ref, sems.at[0]),
-        pltpu.make_async_copy(next_hbm, next_ref, sems.at[1]),
-    ]
-    for copy in copies:
-        copy.start()
-    tokens, width = rows_ref.shape
-    rank = backward_ref.shape[0]
+def factor_kernel(gathered_ref, forward_ref, backward_ref):
+    rank, tokens = forward_ref.shape
     half = tokens // 2
     total = gathered_ref[0].astype(F32)
     for member in range(1, gathered_ref.shape[0]):
@@ -176,20 +167,23 @@
         diagonal = total[mark : mark + 1] + total[mark + 1 : mark + 2]
         gram = unpacked(total[turn * half : (turn + 1) * half], diagonal)
         pairs.append(orthonormal(gram, total[at : at + rank]))
-    forward, backward = (basis.astype(BF16) for basis in eliminate(pairs))
-    backward_ref[...] = backward
-    for copy in copies:
-        copy.wait()
+    forward, backward = eliminate(pairs)
+    forward_ref[...] = forward.astype(BF16)
+    backward_ref[...] = backward.astype(BF16)
+
+
+def local_kernel(basis_ref, rows_ref, grad_ref, spread_ref, local_ref):
+    width = rows_ref.shape[1]
+    basis = basis_ref[...]
     chunk = 1024
     for start in range(0, width, chunk):
-        coeff = jnp.dot(
-            forward, rows_ref[:, start : start + chunk], preferred_element_type=F32
-        ).astype(BF16)
-        other = jnp.dot(forward, next_ref[:, start : start + chunk], preferred_element_type=F32)
+        at = slice(start, start + chunk)
+        coeff = jnp.dot(basis, rows_ref[:, at], preferred_element_type=F32).astype(BF16)
+        other = jnp.dot(basis, grad_ref[:, at], preferred_element_type=F32)
         summed = jnp.sum(coeff.astype(F32) * other, axis=0, keepdims=True)
         for lane in range(0, chunk, 128):
-            at = (start + lane) // 128
-            local_ref[at : at + 1] = summed[:, lane : lane + 128]
+            line = (start + lane) // 128
+            local_ref[line : line + 1] = summed[:, lane : lane + 128]
     local = local_ref[...].astype(BF16)
     for i in range(spread_ref.shape[0]):
         spread_ref[i] = local
@@ -242,25 +236,32 @@
     )(rows, grad, gain, sketch_rows)
 
 
-def factors(gathered, rows, next_grad, rank, copies):
-    tokens, width = rows.shape
+def factors(gathered, rank):
+    tokens = gathered.shape[2]
     vmem = pl.BlockSpec(memory_space=pltpu.VMEM)
-    anywhere = pl.BlockSpec(memory_space=pl.ANY)
     basis = jax.ShapeDtypeStruct((rank, tokens), BF16)
     return pl.pallas_call(
         factor_kernel,
-        out_shape=(jax.ShapeDtypeStruct((copies, width // 128, 128), BF16), basis),
-        in_specs=[vmem, anywhere, anywhere],
+        out_shape=(basis, basis),
+        in_specs=[vmem],
         out_specs=(vmem, vmem),
-        scratch_shapes=[
-            pltpu.VMEM((width // 128, 128), F32),
-            pltpu.VMEM((tokens, width), BF16),
-            pltpu.VMEM((tokens, width), BF16),
-            pltpu.SemaphoreType.DMA((2,)),
-        ],
         compiler_params=SMALL,
         name="factors",
-    )(gathered, rows, next_grad)
+    )(gathered)
+
+
+def local_sums(basis, rows, grad, copies):
+    width = rows.shape[1]
+    vmem = pl.BlockSpec(memory_space=pltpu.VMEM)
+    return pl.pallas_call(
+        local_kernel,
+        out_shape=jax.ShapeDtypeStruct((copies, width // 128, 128), BF16),
+        in_specs=[vmem, vmem, vmem],
+        out_specs=vmem,
+        scratch_shapes=[pltpu.VMEM((width // 128, 128), F32)],
+        compiler_params=SMALL,
+        name="local_sums",
+    )(basis, rows, grad)
 
 
 def coefficients(basis, grad, gain):
@@ -304,15 +305,16 @@
     sketch_rows = sketch_matrix[0].T
     grad = grad_gained[0]
     tokens = rows.shape[0]
-    next_grad = along_section(grad, -1)
+    earlier_rows = along_section(rows, 1)
     mine = partials(rows, grad, boundary_gain, sketch_rows)
     gathered = lax.all_gather(mine, "tensor")
-    local, backward = factors(gathered, rows, next_grad, sketch_rows.shape[0], lax.axis_size("dp"))
+    forward, backward = factors(gathered, sketch_rows.shape[0])
+    forward = along_section(forward, 1)
     both = coefficients(backward, grad, boundary_gain)
     both = along_section(both, -1)
-    locals_ = lax.all_to_all(local, "dp", 0, 0)
-    summed = jnp.sum(locals_.astype(F32), axis=0)
-    gain_grad = along_section(summed, 1)
+    local = local_sums(forward, earlier_rows, grad, lax.axis_size("dp"))
+    parts = lax.all_to_all(local, "dp", 0, 0)
+    gain_grad = jnp.sum(parts.astype(F32), axis=0)
     grad_output = rebuild(both, tokens)
     return grad_output[None], gain_grad.reshape(1, -1)
 

time: 81.4 us -> 81.3 us (level)
  starting transfers between devices: 13 us -> 9.25 us
  blocking collectives: 46.9 us -> 49.7 us
  waiting for transfers between devices: 11.5 us -> 12.6 us
    ppermute x3, waiting for transfers between devices: 3.98 us -> 9.11 us  [along_section(): return lax.ppermute(block, 'section', route)]
    all_to_all x1, waiting for transfers between devices: 7.5 us -> 3.44 us  [shards(): parts = lax.all_to_all(local, 'dp', 0, 0)]
    ppermute x3, starting transfers between devices: 9.27 us -> 5.76 us  [along_section(): return lax.ppermute(block, 'section', route)]
    all_gather x1, blocking collectives: 46.9 us -> 49.7 us  [shards(): gathered = lax.all_gather(mine, 'tensor')]
    pallas_call x1 -> x2, Pallas kernels: 3.13 us -> 2.95 us  [the longest x1 1.9 us: factors(): pl.pallas_call(factor_kernel, out_shape=(basis, basis), in_specs=[vmem],...]
  transfers between devices with their start and end apart: 4 -> 4, of which waited for: 2 -> 3; matrix products, arithmetic and copies ran while one was open for 0% -> 0% of each run, Pallas kernels for 6% -> 9%
where the time goes in v5:
time: 81.3 us; the launch traced here: 81 us
  blocking collectives  49.7 us (61%)
  waiting for transfers between devices  12.6 us (15%)
  starting transfers between devices  9.25 us (11%)
  Pallas kernels  8.16 us (10%)
    all_gather x1, blocking collectives, shards(): gathered = lax.all_gather(mine, 'tensor')  49.7 us
    ppermute x3, waiting for transfers between devices, along_section(): return lax.ppermute(block, 'section', route)  9.11 us
    ppermute x3, starting transfers between devices, along_section(): return lax.ppermute(block, 'section', route)  5.76 us
    pallas_call x1, Pallas kernels, partials(): pl.pallas_call(partials_kernel, out_shape=jax.ShapeDtypeStruct((tokens +...  3.65 us
    all_to_all x1, starting transfers between devices, shards(): parts = lax.all_to_all(local, 'dp', 0, 0)  3.49 us
    all_to_all x1, waiting for transfers between devices, shards(): parts = lax.all_to_all(local, 'dp', 0, 0)  3.44 us
    pallas_call x1, Pallas kernels, factors(): pl.pallas_call(factor_kernel, out_shape=(basis, basis), in_specs=[vmem],...  1.9 us
  transfers between devices with their start and end apart: 4, of which 3 were waited for; matrix products, arithmetic and copies ran while one was open for 0% of the time, Pallas kernels for 9%

profile of v5, /device:TPU:24, one launch (start us, length us, event | category | flops | bytes accessed | tf_op | source)
XLA Modules:
  0.0 81.0 jit_solution(13251097364511761306)
XLA Ops:
  0.6 1.9 %collective-permute-start.2 = (bf16[128,4096]{1,0:T(8,128)(2,1)}, bf16[128,4096]{1,0:T(8,128)(2,1)S(1)}, u32[]{:S(2)}, u32[]{:S(2)}) collective-permute-start(bf16[128,4096]{1,0:T(8,128)(2,1)} %bitcast.13), channel_id=1, source_target_pairs={{0,4},{4,8},{8,12},{12,16},{16,20},{20,24},{24,28},{28,32},{32,36}... | collective-permute-start | bytes 3145736 | tf_op jit(solution)/shard_map/ppermute | solution.py:300
  2.6 0.0 copy-start
  2.6 3.6 %partials.1 = bf16[200,128]{1,0:T(8,128)(2,1)} custom-call(bf16[128,4096]{1,0:T(8,128)(2,1)} %bitcast.14, bf16[128,4096]{1,0:T(8,128)(2,1)} %bitcast.8, bf16[1,4096]{1,0:T(2,128)(2,1)} %gain_ref.1, bf16[32,4096]{1,0:T(8,128)(2,1)} %bitcast.15), custom_call_target="tpu_custom_call" | custom-call | tf_op jit(solution)/shard_map/partials/pallas_call | solution.py:223
  6.2 49.7 %all-gather = bf16[800,128]{1,0:T(8,128)(2,1)S(1)} all-gather(bf16[200,128]{1,0:T(8,128)(2,1)} %partials.1), channel_id=2, replica_groups=mesh['dp'=8,'section'=32,'tensor'=4] {'tensor'}, dimensions={0}, use_global_device_ids=true | all-gather | bytes 256000 | tf_op jit(solution)/shard_map/all_gather | solution.py:310
  55.9 1.9 %factors.1 = (bf16[32,128]{1,0:T(8,128)(2,1)S(1)}, bf16[32,128]{1,0:T(8,128)(2,1)S(1)}) custom-call(bf16[4,200,128]{2,1,0:T(8,128)(2,1)S(1)} %bitcast.11), custom_call_target="tpu_custom_call" | custom-call | tf_op jit(solution)/shard_map/factors/pallas_call | solution.py:243
  57.9 1.9 %collective-permute-start.1 = (bf16[32,128]{1,0:T(8,128)(2,1)S(1)}, bf16[32,128]{1,0:T(8,128)(2,1)S(1)}, u32[]{:S(2)}, u32[]{:S(2)}) collective-permute-start(bf16[32,128]{1,0:T(8,128)(2,1)S(1)} %get-tuple-element.5), channel_id=1, source_target_pairs={{0,4},{4,8},{8,12},{12,16},{16,20},{20,24},{24,28},{28,32},{32,36}... | collective-permute-start | bytes 24584 | tf_op jit(solution)/shard_map/ppermute | solution.py:300
  59.8 5.2 %collective-permute-done.1.basis_ref = bf16[32,128]{1,0:T(8,128)(2,1)S(1)} collective-permute-done((bf16[32,128]{1,0:T(8,128)(2,1)S(1)}, bf16[32,128]{1,0:T(8,128)(2,1)S(1)}, u32[]{:S(2)}, u32[]{:S(2)}) %collective-permute-start.1) | collective-permute-done | bytes 8224 | tf_op jit(solution)/shard_map/ppermute | solution.py:300
  64.9 0.0 collective-permute-done.2.rows_ref
  64.9 0.0 copy-done
  64.9 1.0 %local_sums.1 = bf16[8,32,128]{2,1,0:T(8,128)(2,1)} custom-call(bf16[32,128]{1,0:T(8,128)(2,1)S(1)} %collective-permute-done.1.basis_ref, bf16[128,4096]{1,0:T(8,128)(2,1)S(1)} %collective-permute-done.2.rows_ref, bf16[128,4096]{1,0:T(8,128)(2,1)S(1)} %bitcast.9), custom_call_target="tpu_custom_call" | custom-call | tf_op jit(solution)/shard_map/local_sums/pallas_call | solution.py:256
  66.0 0.0 copy-start.1
  66.0 3.5 %all-to-all-start = ((bf16[8,32,128]{2,1,0:T(8,128)(2,1)}), bf16[8,32,128]{2,1,0:T(8,128)(2,1)S(1)}, u32[]{:S(2)}, u32[]{:S(2)}) async-start(bf16[8,32,128]{2,1,0:T(8,128)(2,1)} %local_sums.1), calls=%async_computation | async-start | bytes 131072 | tf_op jit(solution)/shard_map/all_to_all | solution.py:316
  69.5 0.0 copy-done.1
  69.5 0.3 coefficients.1
  69.8 1.9 %collective-permute-start = (bf16[32,4224]{1,0:T(8,128)(2,1)S(1)}, bf16[32,4224]{1,0:T(8,128)(2,1)S(1)}, u32[]{:S(2)}, u32[]{:S(2)}) collective-permute-start(bf16[32,4224]{1,0:T(8,128)(2,1)S(1)} %coefficients.1), channel_id=1, source_target_pairs={{4,0},{8,4},{12,8},{16,12},{20,16},{24,20},{28,24},{32,28},{36,32}... | collective-permute-start | bytes 811016 | tf_op jit(solution)/shard_map/ppermute | solution.py:300
  71.7 4.0 %collective-permute-done.both_ref = bf16[32,4224]{1,0:T(8,128)(2,1)S(1)} collective-permute-done((bf16[32,4224]{1,0:T(8,128)(2,1)S(1)}, bf16[32,4224]{1,0:T(8,128)(2,1)S(1)}, u32[]{:S(2)}, u32[]{:S(2)}) %collective-permute-start) | collective-permute-done | bytes 270368 | tf_op jit(solution)/shard_map/ppermute | solution.py:300
  75.7 1.2 %rebuild.1 = bf16[128,4096]{1,0:T(8,128)(2,1)} custom-call(bf16[32,4224]{1,0:T(8,128)(2,1)S(1)} %collective-permute-done.both_ref), custom_call_target="tpu_custom_call" | custom-call | tf_op jit(solution)/shard_map/rebuild/pallas_call | solution.py:283
  76.9 3.4 %all-to-all-done = bf16[8,32,128]{2,1,0:T(8,128)(2,1)S(1)} async-done(((bf16[8,32,128]{2,1,0:T(8,128)(2,1)}), bf16[8,32,128]{2,1,0:T(8,128)(2,1)S(1)}, u32[]{:S(2)}, u32[]{:S(2)}) %all-to-all-start) | async-done | bytes 65568 | tf_op jit(solution)/shard_map/all_to_all | solution.py:316
  80.4 0.6 convert_reduce_fusion
Async XLA Ops:
  0.6 64.3 %collective-permute-start.2 = (bf16[128,4096]{1,0:T(8,128)(2,1)}, bf16[128,4096]{1,0:T(8,128)(2,1)S(1)}, u32[]{:S(2)}, u32[]{:S(2)}) collective-permute-start(bf16[128,4096]{1,0:T(8,128)(2,1)} %bitcast.13), channel_id=1, source_target_pairs={{0,4},{4,8},{8,12},{12,16},{16,20},{20,24},{24,28},{28,32},{32,36}... | collective-permute-start | bytes 3145736 | tf_op jit(solution)/shard_map/ppermute | solution.py:300
  2.6 62.4 %copy-start = (bf16[1,128,4096]{2,1,0:T(8,128)(2,1)S(1)}, bf16[1,128,4096]{2,1,0:T(8,128)(2,1)}, u32[]{:S(2)}) copy-start(bf16[1,128,4096]{2,1,0:T(8,128)(2,1)} %param.7) | copy-start | bytes 3145732
  57.9 7.1 %collective-permute-start.1 = (bf16[32,128]{1,0:T(8,128)(2,1)S(1)}, bf16[32,128]{1,0:T(8,128)(2,1)S(1)}, u32[]{:S(2)}, u32[]{:S(2)}) collective-permute-start(bf16[32,128]{1,0:T(8,128)(2,1)S(1)} %get-tuple-element.5), channel_id=1, source_target_pairs={{0,4},{4,8},{8,12},{12,16},{16,20},{20,24},{24,28},{28,32},{32,36}... | collective-permute-start | bytes 24584 | tf_op jit(solution)/shard_map/ppermute | solution.py:300
  66.0 3.5 %copy-start.1 = (bf16[1,4096]{1,0:T(2,128)(2,1)S(1)}, bf16[1,4096]{1,0:T(2,128)(2,1)}, u32[]{:S(2)}) copy-start(bf16[1,4096]{1,0:T(2,128)(2,1)} %gain_ref.1) | copy-start | bytes 24580
  66.0 14.4 %all-to-all-start = ((bf16[8,32,128]{2,1,0:T(8,128)(2,1)}), bf16[8,32,128]{2,1,0:T(8,128)(2,1)S(1)}, u32[]{:S(2)}, u32[]{:S(2)}) async-start(bf16[8,32,128]{2,1,0:T(8,128)(2,1)} %local_sums.1), calls=%async_computation | async-start | bytes 131072 | tf_op jit(solution)/shard_map/all_to_all | solution.py:316
  69.8 5.9 %collective-permute-start = (bf16[32,4224]{1,0:T(8,128)(2,1)S(1)}, bf16[32,4224]{1,0:T(8,128)(2,1)S(1)}, u32[]{:S(2)}, u32[]{:S(2)}) collective-permute-start(bf16[32,4224]{1,0:T(8,128)(2,1)S(1)} %coefficients.1), channel_id=1, source_target_pairs={{4,0},{8,4},{12,8},{16,12},{20,16},{24,20},{28,24},{32,28},{36,32}... | collective-permute-start | bytes 811016 | tf_op jit(solution)/shard_map/ppermute | solution.py:300
